TPU v7x, 32 devices: a whole 2x2x4 slice. The times are simulated.
32 devices in a mesh: row: 8 (over y, x, core), col: 4 (over z).
Axes of the slice: x: 2, y: 2, z: 4, core: 2. Of those that a mesh axis runs over, the one named last changes fastest.
Arguments:
- covariance: float32 [4096, 4096], P('row', 'col'), as said below
- phenotypes: float32 [4096, 512], P('row', 'col'), may hold values from -6 to 6
Outputs:
- updated: float32 [4096, 4096], P('row', 'col')
- solved: float32 [4096, 512], P(('row', 'col'))
Inputs may be any that keep to these rules, and one draw needn't show every extreme that they name: covariance is symmetric and its leading 256 x 256 block is positive definite.
All inputs are finite; a program needn't handle non-finite values.
Results may differ from a plain program's by a relative error of at most 0.00007.
Values sent between devices are 32-bit elements; how exact they have to be, the bound alone decides.
No kernel may reach another device: no remote copies, remote signals or barrier semaphores. Data moves between devices by JAX's collectives and lax.ppermute only.
A program may use at most 64 MiB of HBM per device.

v0:
```python
import jax
import jax.numpy as jnp
from jax import lax
from jax.experimental import pallas as pl
from jax.experimental.pallas import tpu as pltpu
from jax.sharding import PartitionSpec as P


PANEL = 256
HALF = PANEL // 2
PIVOTS = 8
EXACT = lax.Precision.HIGHEST
AXES = ("row", "col")


MIB = 1 << 20
ANYWHERE = pl.BlockSpec(memory_space=pl.ANY)
IN_PLACE = pl.BlockSpec(memory_space=pltpu.HBM)


def grant(mib):
    return pltpu.CompilerParams(vmem_limit_bytes=int(mib * MIB))


def whole(shape):
    return pl.BlockSpec(shape, lambda *_: (0,) * len(shape))


def exact_dot(a, b, ca, cb):
    return lax.dot_general(
        a, b, (((ca,), (cb,)), ((), ())), precision=EXACT, preferred_element_type=jnp.float32
    )


def split(x, terms):
    out = []
    for _ in range(terms):
        out.append(x.astype(jnp.bfloat16))
        x = x - out[-1].astype(jnp.float32)
    return out


def split_dot(a, b, ca, cb):
    total = None
    for order in reversed(range(len(a))):
        for i in range(order + 1):
            part = lax.dot_general(
                a[i], b[order - i], (((ca,), (cb,)), ((), ())), preferred_element_type=jnp.float32
            )
            total = part if total is None else total + part
    return total


def eliminate(block, out_ref):
    n = block.shape[0]
    shape = (PIVOTS, n)
    lane = lax.broadcasted_iota(jnp.int32, shape, 1)
    sub = lax.broadcasted_iota(jnp.int32, shape, 0)
    steps = n // PIVOTS

    def spread(x, k):
        return jnp.broadcast_to(x[:, k : k + 1], shape)

    def row_of(x, i):
        return jnp.broadcast_to(x[i : i + 1, :], shape)

    t = [block[PIVOTS * h : PIVOTS * (h + 1), :] for h in range(steps)]
    pivots = [spread(t[0], j) for j in range(PIVOTS)]
    for g in range(steps):
        k0 = g * PIVOTS
        more = g + 1 < steps
        inside = (lane >= k0) & (lane < k0 + PIVOTS)
        e = [[row_of(pivots[j], i) for j in range(i + 1)] for i in range(PIVOTS)]
        r = [
            jnp.where(inside, jnp.where(lane == k0 + k, 1.0, 0.0), row_of(t[g], k))
            for k in range(PIVOTS)
        ]
        if more:
            c = [spread(t[g + 1], k0 + j) for j in range(PIVOTS)]
            following = [spread(t[g + 1], k0 + PIVOTS + j) for j in range(PIVOTS)]
            rows = jnp.where(inside, 0.0, t[g + 1])
        inv = []
        low = [[None] * PIVOTS for _ in range(PIVOTS)]
        for k in range(PIVOTS):
            inv.append(1.0 / e[k][k])
            for i in range(k + 1, PIVOTS):
                low[i][k] = e[i][k] * inv[k]
                for j in range(k + 1, i + 1):
                    e[i][j] = e[i][j] - low[i][k] * e[j][k]
                r[i] = r[i] - low[i][k] * r[k]
            if more:
                f = c[k] * inv[k]
                for j in range(k + 1, PIVOTS):
                    c[j] = c[j] - f * e[j][k]
                rows = rows - f * r[k]
                for j in range(PIVOTS):
                    following[j] = following[j] - f * row_of(c[k], j)
        done = jnp.zeros(shape, jnp.float32)
        for k in range(PIVOTS):
            done = jnp.where(sub == k, r[k] * lax.rsqrt(e[k][k]), done)
        out_ref[k0 : k0 + PIVOTS, :] = jnp.where(lane < k0 + PIVOTS, done, 0.0)
        if not more:
            break
        t[g + 1] = rows
        pivots = following
        if g + 2 < steps:
            q = [r[k] * inv[k] for k in range(PIVOTS)]
            for k in range(PIVOTS - 1, 0, -1):
                for j in range(k):
                    q[j] = q[j] - low[k][j] * q[k]
            for h in range(g + 2, steps):
                acc = jnp.where(inside, 0.0, t[h])
                for j in range(PIVOTS):
                    acc = acc - spread(t[h], k0 + j) * q[j]
                t[h] = acc


def factor_kernel(d_ref, w_ref, w11_ref, w22_ref):
    m = d_ref.shape[0]
    eliminate(d_ref[:, :m], w11_ref)
    w11 = w11_ref[...]
    l21 = exact_dot(d_ref[:, m : 2 * m], w11, 1, 1)
    rest = d_ref[:, 2 * m :] - exact_dot(l21, l21, 1, 1)
    below = exact_dot(l21, w11, 1, 0)
    eliminate(rest, w22_ref)
    w22 = w22_ref[...]
    w_ref[:, :m] = w11
    w_ref[:, m : 2 * m] = -exact_dot(w22, below, 1, 0)
    w_ref[:, 2 * m :] = w22


def factor_inverse(blocks):
    m = blocks.shape[0]
    return pl.pallas_call(
        factor_kernel,
        out_shape=jax.ShapeDtypeStruct(blocks.shape, jnp.float32),
        scratch_shapes=[pltpu.VMEM((m, m), jnp.float32)] * 2,
        compiler_params=grant(4),
        cost_estimate=pl.CostEstimate(flops=1 << 32, bytes_accessed=1 << 19, transcendentals=0),
    )(blocks)


def full_inverse(w_ref, out_ref):
    m = w_ref.shape[0]
    out_ref[:m, :m] = w_ref[:, :m]
    out_ref[:m, m:] = jnp.zeros((m, m), jnp.float32)
    out_ref[m:, :] = w_ref[:, m:]


def lead_kernel(cov_ref, out_ref, sem):
    copies = []
    for i, (r, c) in enumerate(((0, 0), (1, 0), (1, 1))):
        source = cov_ref.at[pl.ds(r * HALF, HALF), pl.ds(c * HALF, HALF)]
        copies.append(pltpu.make_async_copy(source, out_ref.at[:, pl.ds(i * HALF, HALF)], sem.at[i]))
    for copy in copies:
        copy.start()
    for copy in copies:
        copy.wait()


def lead_blocks(covariance):
    return pl.pallas_call(
        lead_kernel,
        in_specs=[IN_PLACE],
        out_shape=jax.ShapeDtypeStruct((HALF, 3 * HALF), jnp.float32),
        scratch_shapes=[pltpu.SemaphoreType.DMA((3,))],
        compiler_params=grant(63),
        cost_estimate=pl.CostEstimate(flops=0, bytes_accessed=1 << 19, transcendentals=0),
    )(covariance)


def payload_kernel(ratio, cov_ref, pheno_ref, *refs):
    out_refs, (rows_ref, head_ref, sem) = refs[:ratio], refs[ratio:]
    piece = out_refs[0].shape[1]
    copies = [
        pltpu.make_async_copy(pheno_ref.at[pl.ds(0, PANEL), :], head_ref, sem.at[0]),
        pltpu.make_async_copy(cov_ref.at[:, pl.ds(0, PANEL)], rows_ref, sem.at[1]),
    ]
    for m in range(ratio):
        source = cov_ref.at[pl.ds(0, PANEL), pl.ds(m * piece, piece)]
        copies.append(pltpu.make_async_copy(source, out_refs[m].at[pl.ds(0, PANEL), :], sem.at[2 + m]))
    for copy in copies:
        copy.start()
    copies[0].wait()
    traits = head_ref.shape[1]
    height = out_refs[0].shape[0] - PANEL
    at = 0
    for m in range(ratio):
        for i in range(piece // traits):
            out_refs[m][PANEL:, i * traits : (i + 1) * traits] = head_ref[at : at + height, :]
            at += height
    for copy in copies[1:]:
        copy.wait()


def payloads(covariance, phenotypes, ratio):
    n, width = covariance.shape
    traits = phenotypes.shape[1]
    piece = width // ratio
    height = PANEL // ratio // (piece // traits)
    out = jax.ShapeDtypeStruct((PANEL + height, piece), jnp.float32)
    return pl.pallas_call(
        lambda *refs: payload_kernel(ratio, *refs),
        in_specs=[IN_PLACE] * 2,
        out_shape=[out] * ratio + [jax.ShapeDtypeStruct((n, PANEL), jnp.float32)],
        scratch_shapes=[pltpu.VMEM((PANEL, traits), jnp.float32), pltpu.SemaphoreType.DMA((2 + ratio,))],
        compiler_params=grant(61.75),
        cost_estimate=pl.CostEstimate(flops=0, bytes_accessed=4 * MIB, transcendentals=0),
    )(covariance, phenotypes)


def rows_kernel(index_of, *refs):
    options, slab_ref, out_ref, sem = refs[:-3], refs[-3], refs[-2], refs[-1]
    index = index_of(lax.axis_index("row"), lax.axis_index("col"))
    for i, option in enumerate(options):

        @pl.when(index == i)
        def _(option=option):
            copy = pltpu.make_async_copy(option, out_ref, sem)
            copy.start()
            copy.wait()

    @pl.when(index == len(options))
    def _():
        for h in range(0, slab_ref.shape[1], HALF):
            out_ref[h : h + HALF, :] = slab_ref[:, h : h + HALF].T


def pick_rows(index_of, options, slab):
    shape = options[0].shape
    return pl.pallas_call(
        lambda *refs: rows_kernel(index_of, *refs),
        grid=(1,),
        in_specs=[ANYWHERE] * len(options) + [pl.BlockSpec((PANEL, slab.shape[1]), lambda *_: (0, 0))],
        out_specs=whole(shape),
        out_shape=jax.ShapeDtypeStruct(shape, jnp.float32),
        scratch_shapes=[pltpu.SemaphoreType.DMA(())],
        compiler_params=grant(6),
        cost_estimate=pl.CostEstimate(flops=0, bytes_accessed=2 * MIB, transcendentals=0),
    )(*options, slab)


def partner(c, s, col_size):
    return c ^ s if col_size & (col_size - 1) == 0 else lax.rem(c + s, col_size)


def from_partner(p, c, col_size):
    return c ^ p if col_size & (col_size - 1) == 0 else lax.rem(c - p + col_size, col_size)


def solve_kernel(col_size, ratio, *refs):
    w_ref, rows_ref, pheno_ref = refs[:3]
    lead_refs = refs[3 : 3 + ratio]
    panel_ref = refs[3 + ratio]
    part_refs = refs[4 + ratio : 4 + ratio + col_size]
    inv_ref, head_ref, left_ref = refs[4 + ratio + col_size :]
    row, col = lax.axis_index("row"), lax.axis_index("col")
    member = lax.rem(row, ratio)
    head_share = PANEL // ratio
    traits = head_ref.shape[1]
    for s in range(ratio):
        first = lax.rem(member - s + ratio, ratio) * head_share
        height, width = lead_refs[s].shape
        for i in range(width // traits):
            at = pl.multiple_of(first + i * height, 8)
            head_ref[pl.ds(at, height), :] = lead_refs[s][:, i * traits : (i + 1) * traits]
    full_inverse(w_ref, inv_ref)
    inverse = split(inv_ref[...], 3)
    head = split_dot(inverse, split(head_ref[...], 3), 1, 0)
    panel = split_dot(split(rows_ref[...], 3), inverse, 1, 1)
    panel_ref[...] = panel
    left_ref[...] = pheno_ref[...] - split_dot(split(panel, 2), split(head, 2), 1, 0)

    @pl.when(row == 0)
    def _():
        left_ref[:PANEL, :] = head

    share = left_ref.shape[0] // col_size
    for s in range(col_size):
        at = pl.multiple_of(partner(col, s, col_size) * share, share)
        part_refs[s][...] = left_ref[pl.ds(at, share), :]


def solve_rows(blocks, rows, pheno, slabs, col_size):
    n, traits = pheno.shape
    ratio = len(slabs)
    height = slabs[0].shape[0] - PANEL
    part = jax.ShapeDtypeStruct((n // col_size, traits), jnp.float32)
    lead = pl.BlockSpec((height, slabs[0].shape[1]), lambda *_: (PANEL // height, 0))
    outs = [jax.ShapeDtypeStruct(rows.shape, jnp.float32)] + [part] * col_size
    return pl.pallas_call(
        lambda *refs: solve_kernel(col_size, ratio, *refs),
        grid=(1,),
        in_specs=[whole(blocks.shape), whole(rows.shape), whole(pheno.shape)] + [lead] * ratio,
        out_specs=[whole(o.shape) for o in outs],
        out_shape=outs,
        scratch_shapes=[
            pltpu.VMEM((PANEL, PANEL), jnp.float32),
            pltpu.VMEM((PANEL, traits), jnp.float32),
            pltpu.VMEM(pheno.shape, jnp.float32),
        ],
        compiler_params=grant(12),
        cost_estimate=pl.CostEstimate(flops=1 << 30, bytes_accessed=1 << 21, transcendentals=0),
    )(blocks, rows, pheno, *slabs)


def trailing_kernel(ratio, *refs):
    w_ref, panel_ref, cov_ref = refs[:3]
    slab_refs = refs[3 : 3 + ratio]
    out_ref, inv_ref, high_ref, low_ref = refs[3 + ratio :]
    row, col = lax.axis_index("row"), lax.axis_index("col")
    member = lax.rem(row, ratio)
    step = pl.program_id(0)

    @pl.when(step == 0)
    def _():
        full_inverse(w_ref, inv_ref)
        inverse = split(inv_ref[...], 3)
        for s in range(ratio):
            piece = slab_refs[s].shape[1]
            first = lax.rem(member - s + ratio, ratio) * piece
            for h in range(0, piece, PANEL):
                right = split_dot(inverse, split(slab_refs[s][:, h : h + PANEL], 3), 1, 0)
                at = pl.ds(pl.multiple_of(first + h, PANEL), PANEL)
                high_ref[:, at], low_ref[:, at] = split(right, 2)

    panel = panel_ref[...]
    lead = (row == 0) & (step * panel.shape[0] < PANEL)
    below = jnp.where(lead, 0.0, panel)
    right = [high_ref[...], low_ref[...]]
    out_ref[...] = cov_ref[...] - split_dot(split(below, 2), right, 1, 0)

    @pl.when(col == 0)
    def _():
        out_ref[:, :PANEL] = panel


def trailing_update(blocks, panel, covariance, slabs):
    n, width = covariance.shape
    ratio = len(slabs)
    tall = min(n, PANEL)
    slab = pl.BlockSpec((PANEL, slabs[0].shape[1]), lambda i: (0, 0))
    return pl.pallas_call(
        lambda *refs: trailing_kernel(ratio, *refs),
        grid=(n // tall,),
        in_specs=[
            whole(blocks.shape),
            pl.BlockSpec((tall, PANEL), lambda i: (i, 0)),
            pl.BlockSpec((tall, width), lambda i: (i, 0)),
        ]
        + [slab] * ratio,
        out_specs=pl.BlockSpec((tall, width), lambda i: (i, 0)),
        out_shape=jax.ShapeDtypeStruct(covariance.shape, jnp.float32),
        scratch_shapes=[
            pltpu.VMEM((PANEL, PANEL), jnp.float32),
            pltpu.VMEM((PANEL, width), jnp.bfloat16),
            pltpu.VMEM((PANEL, width), jnp.bfloat16),
        ],
        compiler_params=grant(16),
        cost_estimate=pl.CostEstimate(flops=1 << 31, bytes_accessed=6 << 20, transcendentals=0),
    )(blocks, panel, covariance, *slabs)


def tree(nodes, level, levels, edges):
    if len(nodes) < 2:
        return
    half = len(nodes) // 2
    edges.append((level, levels[nodes[0]], nodes[0], nodes[half]))
    levels[nodes[half]] = level
    tree(nodes[:half], level + 1, levels, edges)
    tree(nodes[half:], level + 1, levels, edges)


def bit_reversed(count):
    bits = max(count - 1, 0).bit_length()
    order = [int(format(i, "0%db" % bits)[::-1], 2) if bits else 0 for i in range(1 << bits)]
    return [i for i in order if i < count]


def choose(index, options):
    out = options[0]
    for i in range(1, len(options)):
        out = jnp.where(index == i, options[i], out)
    return out


def look_up(table, at):
    out = table[0]
    for i, value in enumerate(table):
        if value != table[0]:
            out = jnp.where(at == i, value, out)
    return out


def shards(covariance, phenotypes):
    row_size, col_size = lax.axis_size("row"), lax.axis_size("col")
    row_index, col_index = lax.axis_index("row"), lax.axis_index("col")
    ratio = row_size // col_size
    groups = row_size // ratio
    group, member = row_index // ratio, lax.rem(row_index, ratio)

    def place(r, c):
        return r * col_size + c

    def send(x, pairs):
        return lax.ppermute(x, AXES, [(place(*a), place(*b)) for a, b in pairs])

    every_group = [(k, c) for k in range(groups) for c in range(col_size)]

    blocks = lead_blocks(covariance)
    found = []
    tree(list(range(col_size)), 1, {0: 0}, found)
    steps = {}
    for lv, sl, s, d in found:
        steps.setdefault(lv, []).append((s, d))
    diag = blocks
    for lv in sorted(steps):
        got = send(diag, [((0, s), (0, d)) for s, d in steps[lv]])
        new = [int(c in [d for _, d in steps[lv]]) for c in range(col_size)]
        diag = jnp.where(look_up(new, col_index) > 0, got, diag)

    *pieces, own_rows = payloads(covariance, phenotypes, ratio)
    start = [pieces[0]]
    for m in range(1, ratio):
        start.append(send(pieces[m], [((0, c), (m, c)) for c in range(col_size)]))
    start = choose(row_index, start)
    stages = {}
    came = {}
    for m in range(ratio):
        nodes = list(range(groups)) if m % 2 == 0 else bit_reversed(groups)
        found = []
        tree(nodes, 1, {0: 0}, found)
        for lv, sl, a, b in found:
            stages.setdefault((lv, sl), []).append((a * ratio + m, b * ratio + m))
            came[b * ratio + m] = (lv, sl)
    keys = sorted(stages)
    results = [start]
    held = {0: start}
    for key in keys:
        pairs = [((a, c), (b, c)) for a, b in stages[key] for c in range(col_size)]
        got = send(held[key[1]], pairs)
        results.append(got)
        if key[0] in held:
            here = [int(came.get(r) == key) for r in range(row_size)]
            held[key[0]] = jnp.where(look_up(here, row_index) > 0, got, held[key[0]])
        else:
            held[key[0]] = got
    source = look_up([keys.index(came[r]) + 1 if r in came else 0 for r in range(row_size)], row_index)

    relay_from = col_size // 2
    targets = []
    for r in range(row_size):
        k = r // ratio
        if k:
            line = [c for c in range(1, col_size) if c != k]
        else:
            line = [relay_from] + [c for c in range(1, col_size - 1) if c != relay_from]
        targets.append(line)
    arrived = []
    for j in range(col_size - 2):
        arrived.append(send(own_rows, [((r, 0), (r, targets[r][j])) for r in range(row_size) if j < len(targets[r])]))

    inverse = factor_inverse(diag)
    got = [inverse]
    for k in range(1, groups):
        got.append(send(inverse, [((0, c), (k * ratio, c)) for c in range(col_size)]))
    inverse = choose(group, got)

    arrived.append(send(arrived[0], [((r, relay_from), (r, col_size - 1)) for r in range(ratio)]))
    mine = choose(source, results)
    slabs = [mine]
    for s in range(1, ratio):
        slabs.append(
            send(
                mine,
                [((k * ratio + m, c), (k * ratio + (m + s) % ratio, c)) for k, c in every_group for m in range(ratio)],
            )
        )

    def index_of(row, col):
        k = row // ratio
        first = jnp.where(
            col == relay_from,
            1,
            jnp.where(col == col_size - 1, col_size - 1, jnp.where(col < relay_from, col + 1, col)),
        )
        later = jnp.where(col == k, col_size, jnp.where(col < k, col, col - 1))
        return jnp.where(col == 0, 0, jnp.where(k == 0, first, later))

    panel_raw = pick_rows(index_of, [own_rows] + arrived, mine)

    got = [inverse]
    for m in range(1, ratio):
        got.append(send(inverse, [((k * ratio, c), (k * ratio + m, c)) for k, c in every_group]))
    inverse = choose(member, got)

    panel, *parts = solve_rows(inverse, panel_raw, phenotypes, slabs, col_size)
    gathered = [parts[0]]
    for s in range(1, col_size):
        pairs = [((r, c), (r, int(partner(c, s, col_size)))) for r in range(row_size) for c in range(col_size)]
        gathered.append(send(parts[s], pairs))
    updated = trailing_update(inverse, panel, covariance, slabs)
    solved = jnp.concatenate(
        [choose(from_partner(p, col_index, col_size), gathered) for p in range(col_size)], axis=1
    )
    return (updated, solved)


def solution(mesh):
    placed = (P("row", "col"), P("row", "col"))

    return jax.shard_map(
        shards,
        mesh=mesh,
        in_specs=placed,
        out_specs=(P("row", "col"), P(("row", "col"), None)),
        check_vma=False,
    )
```

profile of v0, /device:TPU:0, one launch (start us, length us, event | category | flops | bytes accessed | tf_op | source)
XLA Modules:
  0.0 60.6 jit_solution(463898299882727094)
XLA Ops:
  0.6 2.7 %shard_map.43 = (f32[288,512]{1,0:T(8,128)}, f32[288,512]{1,0:T(8,128)}, f32[512,256]{1,0:T(8,128)}) custom-call(f32[512,1024]{1,0:T(8,128)} %refs_2_.3, f32[512,128]{1,0:T(8,128)} %refs_2_.2), custom_call_target="tpu_custom_call" | custom-call | bytes 4194304 | tf_op jit(solution)/shard_map/pallas_call | solution.py:202
  3.3 0.0 copy-start.1
  3.3 3.4 %collective-permute-start.9 = (f32[288,512]{1,0:T(8,128)}, f32[288,512]{1,0:T(8,128)}, u32[]{:S(2)}, u32[]{:S(2)}) collective-permute-start(f32[288,512]{1,0:T(8,128)} %get-tuple-element.11), channel_id=1, source_target_pairs={{0,4},{1,5},{2,6},{3,7}} | collective-permute-start | bytes 1769480 | tf_op jit(solution)/shard_map/ppermute | solution.py:406
  6.7 1.6 %shard_map.41 = f32[128,384]{1,0:T(8,128)} custom-call(f32[512,1024]{1,0:T(8,128)} %refs_2_.3), custom_call_target="tpu_custom_call" | custom-call | bytes 524288 | tf_op jit(solution)/shard_map/pallas_call | solution.py:162
  8.3 5.3 %collective-permute-start = (f32[128,384]{1,0:T(8,128)}, f32[128,384]{1,0:T(8,128)S(1)}, u32[]{:S(2)}, u32[]{:S(2)}) collective-permute-start(f32[128,384]{1,0:T(8,128)} %shard_map.41), channel_id=1, source_target_pairs={{0,2}} | collective-permute-start | bytes 589832 | tf_op jit(solution)/shard_map/ppermute | solution.py:406
  13.7 0.0 collective-permute-done.9
  13.7 1.2 %broadcast_select_fusion = f32[288,512]{1,0:T(8,128)S(1)} fusion(f32[288,512]{1,0:T(8,128)} %collective-permute-done.9, f32[288,512]{1,0:T(8,128)} %get-tuple-element.12, pred[]{:T(512)S(6)} %eq.95), kind=kLoop, calls=%fused_computation.1 | loop fusion | flops 147456 | bytes 1769473 | tf_op jit(solution)/shard_map/jit(_where)/select_n | solution.py:383
  14.8 0.0 copy-start.3
  14.8 2.1 %collective-permute-start.10 = (f32[288,512]{1,0:T(8,128)S(1)}, f32[288,512]{1,0:T(8,128)}, u32[]{:S(2)}, u32[]{:S(2)}) collective-permute-start(f32[288,512]{1,0:T(8,128)S(1)} %broadcast_select_fusion), channel_id=1, source_target_pairs={{0,16},{1,17},{2,18},{3,19},{4,12},{5,13},{6,14},{7,15}} | collective-permute-start | bytes 1769480 | tf_op jit(solution)/shard_map/ppermute | solution.py:406
  17.0 0.1 collective-permute-done
  17.1 0.9 %broadcast_select_fusion.1 = f32[128,384]{1,0:T(8,128)S(1)} fusion(f32[128,384]{1,0:T(8,128)S(1)} %collective-permute-done, f32[128,384]{1,0:T(8,128)} %shard_map.41, pred[]{:T(512)S(6)} %gt.7), kind=kLoop, calls=%fused_computation.4 | loop fusion | flops 49152 | bytes 589825 | tf_op jit(solution)/shard_map/jit(_where)/select_n | solution.py:420
  18.1 1.3 %collective-permute-start.1 = (f32[128,384]{1,0:T(8,128)S(1)}, f32[128,384]{1,0:T(8,128)S(1)}, u32[]{:S(2)}, u32[]{:S(2)}) collective-permute-start(f32[128,384]{1,0:T(8,128)S(1)} %broadcast_select_fusion.1), channel_id=1, source_target_pairs={{0,1},{2,3}} | collective-permute-start | bytes 589832 | tf_op jit(solution)/shard_map/ppermute | solution.py:406
  19.4 0.0 copy-done.1
  19.4 4.3 %collective-permute-start.6 = (f32[512,256]{1,0:T(8,128)S(1)}, f32[512,256]{1,0:T(8,128)S(1)}, u32[]{:S(2)}, u32[]{:S(2)}) collective-permute-start(f32[512,256]{1,0:T(8,128)S(1)} %copy-done.1), channel_id=1, source_target_pairs={{0,2},{4,6},{8,10},{12,14},{16,17},{20,21},{24,25},{28,29}} | collective-permute-start | bytes 1572872 | tf_op jit(solution)/shard_map/ppermute | solution.py:406
  23.7 1.3 %collective-permute-start.7 = (f32[512,256]{1,0:T(8,128)S(1)}, f32[512,256]{1,0:T(8,128)S(1)}, u32[]{:S(2)}, u32[]{:S(2)}) collective-permute-start(f32[512,256]{1,0:T(8,128)S(1)} %copy-done.1), channel_id=1, source_target_pairs={{0,1},{4,5},{8,11},{12,15},{16,19},{20,23},{24,26},{28,30}} | collective-permute-start | bytes 1572872 | tf_op jit(solution)/shard_map/ppermute | solution.py:406
  25.1 1.3 %collective-permute-start.12 = (f32[288,512]{1,0:T(8,128)S(1)}, f32[288,512]{1,0:T(8,128)S(1)}, u32[]{:S(2)}, u32[]{:S(2)}) collective-permute-start(f32[288,512]{1,0:T(8,128)S(1)} %broadcast_select_fusion), channel_id=1, source_target_pairs={{0,8},{1,9},{2,10},{3,11},{4,20},{5,21},{6,22},{7,23}} | collective-permute-start | bytes 1769480 | tf_op jit(solution)/shard_map/ppermute | solution.py:406
  26.4 0.0 collective-permute-done.10
  26.4 0.7 %collective-permute-start.11 = (f32[288,512]{1,0:T(8,128)}, f32[288,512]{1,0:T(8,128)S(1)}, u32[]{:S(2)}, u32[]{:S(2)}) collective-permute-start(f32[288,512]{1,0:T(8,128)} %collective-permute-done.10), channel_id=1, source_target_pairs={{16,24},{17,25},{18,26},{19,27},{12,28},{13,29},{14,30},{15,31}} | collective-permute-start | bytes 1769480 | tf_op jit(solution)/shard_map/ppermute | solution.py:406
  27.1 0.0 collective-permute-done.1
  27.2 6.5 %shard_map.42 = f32[128,384]{1,0:T(8,128)S(1)} custom-call(f32[128,384]{1,0:T(8,128)S(1)} %broadcast_select_fusion.2.d_ref), custom_call_target="tpu_custom_call" | custom-call | flops 4294967296 | bytes 524288 | tf_op jit(solution)/shard_map/pallas_call | solution.py:134
  33.7 0.0 copy-done.3
  33.7 1.3 %collective-permute-start.2 = (f32[128,384]{1,0:T(8,128)S(1)}, f32[128,384]{1,0:T(8,128)S(1)}, u32[]{:S(2)}, u32[]{:S(2)}) collective-permute-start(f32[128,384]{1,0:T(8,128)S(1)} %shard_map.42), channel_id=1, source_target_pairs={{0,24},{1,25},{2,26},{3,27}} | collective-permute-start | bytes 589832 | tf_op jit(solution)/shard_map/ppermute | solution.py:406
  35.0 0.9 %collective-permute-done.6.refs_1_ = f32[512,256]{1,0:T(8,128)S(1)} collective-permute-done((f32[512,256]{1,0:T(8,128)S(1)}, f32[512,256]{1,0:T(8,128)S(1)}, u32[]{:S(2)}, u32[]{:S(2)}) %collective-permute-start.6) | collective-permute-done | bytes 524320 | tf_op jit(solution)/shard_map/ppermute | solution.py:406
  36.0 1.7 %collective-permute-start.3 = (f32[128,384]{1,0:T(8,128)S(1)}, f32[128,384]{1,0:T(8,128)S(1)}, u32[]{:S(2)}, u32[]{:S(2)}) collective-permute-start(f32[128,384]{1,0:T(8,128)S(1)} %shard_map.42), channel_id=1, source_target_pairs={{0,16},{1,17},{2,18},{3,19}} | collective-permute-start | bytes 589832 | tf_op jit(solution)/shard_map/ppermute | solution.py:406
  37.7 0.0 collective-permute-done.12
  37.7 1.3 %collective-permute-start.4 = (f32[128,384]{1,0:T(8,128)S(1)}, f32[128,384]{1,0:T(8,128)S(1)}, u32[]{:S(2)}, u32[]{:S(2)}) collective-permute-start(f32[128,384]{1,0:T(8,128)S(1)} %shard_map.42), channel_id=1, source_target_pairs={{0,8},{1,9},{2,10},{3,11}} | collective-permute-start | bytes 589832 | tf_op jit(solution)/shard_map/ppermute | solution.py:406
  39.0 0.0 collective-permute-done.11
  39.0 0.7 %collective-permute-start.8 = (f32[512,256]{1,0:T(8,128)S(1)}, f32[512,256]{1,0:T(8,128)S(1)}, u32[]{:S(2)}, u32[]{:S(2)}) collective-permute-start(f32[512,256]{1,0:T(8,128)S(1)} %collective-permute-done.6.refs_1_), channel_id=1, source_target_pairs={{2,3},{6,7}} | collective-permute-start | bytes 1572872 | tf_op jit(solution)/shard_map/ppermute | solution.py:406
  39.7 1.3 %select_select_fusion.refs_4_.refs_3_ = f32[288,512]{1,0:T(8,128)S(1)} fusion(f32[288,512]{1,0:T(8,128)S(1)} %collective-permute-done.11, f32[288,512]{1,0:T(8,128)S(1)} %collective-permute-done.12, f32[288,512]{1,0:T(8,128)} %collective-permute-done.10, f32[288,512]{1,0:T(8,128)} %copy-done.3, pred[]{:T(512)S(6)} %eq.97, pred[]{:T(512)S(6)} %eq.96, pred[]{:T(512)S(6)} %eq.94), kind=kLoop, calls=%fused_computation | loop fusion | flops 442368 | bytes 2949123 | tf_op jit(solution)/shard_map/jit(_where)/select_n | solution.py:383
  41.1 0.0 collective-permute-done.2
  41.1 0.1 collective-permute-start.13
  41.1 0.0 collective-permute-done.3
  41.2 1.0 %collective-permute-done.4 = f32[128,384]{1,0:T(8,128)S(1)} collective-permute-done((f32[128,384]{1,0:T(8,128)S(1)}, f32[128,384]{1,0:T(8,128)S(1)}, u32[]{:S(2)}, u32[]{:S(2)}) %collective-permute-start.4) | collective-permute-done | bytes 196640 | tf_op jit(solution)/shard_map/ppermute | solution.py:406
  42.2 0.0 copy-start.2
  42.2 1.5 %collective-permute-start.5 = (f32[128,384]{1,0:T(8,128)S(1)}, f32[128,384]{1,0:T(8,128)S(1)}, u32[]{:S(2)}, u32[]{:S(2)}) collective-permute-start(f32[128,384]{1,0:T(8,128)S(1)} %select_select_fusion.1), channel_id=1, source_target_pairs={{0,4},{1,5},{2,6},{3,7},{8,12},{9,13},{10,14},{11,15},{16,20},{17,... | collective-permute-start | bytes 589832 | tf_op jit(solution)/shard_map/ppermute | solution.py:406
  43.8 1.0 %collective-permute-done.5 = f32[128,384]{1,0:T(8,128)S(1)} collective-permute-done((f32[128,384]{1,0:T(8,128)S(1)}, f32[128,384]{1,0:T(8,128)S(1)}, u32[]{:S(2)}, u32[]{:S(2)}) %collective-permute-start.5) | collective-permute-done | bytes 196640 | tf_op jit(solution)/shard_map/ppermute | solution.py:406
  44.8 0.0 collective-permute-done.7.refs_2_
  44.8 0.0 collective-permute-done.8.refs_3_
  44.8 0.1 shard_map.44.refs_1_
  44.9 0.0 copy-start
  45.0 0.0 collective-permute-done.13.refs_4_
  45.0 0.0 copy-done.2
  45.0 2.4 %shard_map.45 = (f32[512,256]{1,0:T(8,128)S(1)}, f32[128,128]{1,0:T(8,128)S(1)}, f32[128,128]{1,0:T(8,128)S(1)}, f32[128,128]{1,0:T(8,128)S(1)}, f32[128,128]{1,0:T(8,128)S(1)}) custom-call(f32[128,384]{1,0:T(8,128)S(1)} %broadcast_select_fusion.3.refs_0_, f32[512,256]{1,0:T(8,128)S(1)} %shard_map.44.refs_1_, f32[512,128]{1,0:T(8,128)S(1)} %copy-done.2, ...), custom_call_target="tpu_custom_call" | custom-call | flops 1073741824 | bytes 2097152 | tf_op jit(solution)/shard_map/pallas_call | solution.py:291
  47.4 7.3 %collective-permute-start.14 = (f32[128,128]{1,0:T(8,128)S(1)}, f32[128,128]{1,0:T(8,128)S(1)}, u32[]{:S(2)}, u32[]{:S(2)}) collective-permute-start(f32[128,128]{1,0:T(8,128)S(1)} %get-tuple-element.14), channel_id=1, source_target_pairs={{0,3},{1,2},{2,1},{3,0},{4,7},{5,6},{6,5},{7,4},{8,11},{9,10},{10,... | collective-permute-start | bytes 196616 | tf_op jit(solution)/shard_map/ppermute | solution.py:406
  54.6 0.0 collective-permute-start.15
  54.6 0.6 %collective-permute-start.16 = (f32[128,128]{1,0:T(8,128)S(1)}, f32[128,128]{1,0:T(8,128)S(1)}, u32[]{:S(2)}, u32[]{:S(2)}) collective-permute-start(f32[128,128]{1,0:T(8,128)S(1)} %get-tuple-element.16), channel_id=1, source_target_pairs={{0,1},{1,0},{2,3},{3,2},{4,5},{5,4},{6,7},{7,6},{8,9},{9,8},{10,11... | collective-permute-start | bytes 196616 | tf_op jit(solution)/shard_map/ppermute | solution.py:406
  55.3 0.0 copy-done
  55.3 4.3 %shard_map.46 = f32[512,1024]{1,0:T(8,128)} custom-call(f32[128,384]{1,0:T(8,128)S(1)} %broadcast_select_fusion.3.refs_0_, f32[512,256]{1,0:T(8,128)S(1)} %get-tuple-element.13.refs_1_, f32[512,1024]{1,0:T(8,128)S(1)} %copy-done, f32[288,512]{1,0:T(8,128)S(1)} %select_select_fusion.refs_4_.refs_3_, f32[288,512]{1,0:T(8,128)} %collective-permute-done.13.refs_4_), custom_call_target="tpu_custom_call" | custom-call | flops 2147483648 | bytes 6291456 | tf_op jit(solution)/shard_map/pallas_call | solution.py:343
  59.5 0.0 collective-permute-done.14
  59.5 0.3 collective-permute-done.15
  59.8 0.0 collective-permute-done.16
  59.8 0.7 %pad_maximum_fusion = f32[128,512]{1,0:T(8,128)} fusion(f32[128,128]{1,0:T(8,128)S(1)} %get-tuple-element.19, f32[128,128]{1,0:T(8,128)S(1)} %get-tuple-element.20, f32[128,128]{1,0:T(8,128)S(1)} %get-tuple-element.21, f32[128,128]{1,0:T(8,128)S(1)} %get-tuple-element.18), kind=kLoop, calls=%fused_computation.2 | loop fusion | flops 196608 | bytes 524288 | tf_op jit(solution)/shard_map/concatenate | solution.py:503
  (4 shorter events, 0.1 us)
Async XLA Ops:
  3.3 16.1 %copy-start.1 = (f32[512,256]{1,0:T(8,128)S(1)}, f32[512,256]{1,0:T(8,128)}, u32[]{:S(2)}) copy-start(f32[512,256]{1,0:T(8,128)} %get-tuple-element.10.refs_0_) | copy-start | bytes 1572868
  3.3 10.3 %collective-permute-start.9 = (f32[288,512]{1,0:T(8,128)}, f32[288,512]{1,0:T(8,128)}, u32[]{:S(2)}, u32[]{:S(2)}) collective-permute-start(f32[288,512]{1,0:T(8,128)} %get-tuple-element.11), channel_id=1, source_target_pairs={{0,4},{1,5},{2,6},{3,7}} | collective-permute-start | bytes 1769480 | tf_op jit(solution)/shard_map/ppermute | solution.py:406
  8.3 8.8 %collective-permute-start = (f32[128,384]{1,0:T(8,128)}, f32[128,384]{1,0:T(8,128)S(1)}, u32[]{:S(2)}, u32[]{:S(2)}) collective-permute-start(f32[128,384]{1,0:T(8,128)} %shard_map.41), channel_id=1, source_target_pairs={{0,2}} | collective-permute-start | bytes 589832 | tf_op jit(solution)/shard_map/ppermute | solution.py:406
  14.8 18.9 %copy-start.3 = (f32[288,512]{1,0:T(8,128)}, f32[288,512]{1,0:T(8,128)S(1)}, u32[]{:S(2)}) copy-start(f32[288,512]{1,0:T(8,128)S(1)} %broadcast_select_fusion) | copy-start | bytes 1769476
  14.8 11.6 %collective-permute-start.10 = (f32[288,512]{1,0:T(8,128)S(1)}, f32[288,512]{1,0:T(8,128)}, u32[]{:S(2)}, u32[]{:S(2)}) collective-permute-start(f32[288,512]{1,0:T(8,128)S(1)} %broadcast_select_fusion), channel_id=1, source_target_pairs={{0,16},{1,17},{2,18},{3,19},{4,12},{5,13},{6,14},{7,15}} | collective-permute-start | bytes 1769480 | tf_op jit(solution)/shard_map/ppermute | solution.py:406
  18.1 9.1 %collective-permute-start.1 = (f32[128,384]{1,0:T(8,128)S(1)}, f32[128,384]{1,0:T(8,128)S(1)}, u32[]{:S(2)}, u32[]{:S(2)}) collective-permute-start(f32[128,384]{1,0:T(8,128)S(1)} %broadcast_select_fusion.1), channel_id=1, source_target_pairs={{0,1},{2,3}} | collective-permute-start | bytes 589832 | tf_op jit(solution)/shard_map/ppermute | solution.py:406
  19.4 16.6 %collective-permute-start.6 = (f32[512,256]{1,0:T(8,128)S(1)}, f32[512,256]{1,0:T(8,128)S(1)}, u32[]{:S(2)}, u32[]{:S(2)}) collective-permute-start(f32[512,256]{1,0:T(8,128)S(1)} %copy-done.1), channel_id=1, source_target_pairs={{0,2},{4,6},{8,10},{12,14},{16,17},{20,21},{24,25},{28,29}} | collective-permute-start | bytes 1572872 | tf_op jit(solution)/shard_map/ppermute | solution.py:406
  23.7 21.1 %collective-permute-start.7 = (f32[512,256]{1,0:T(8,128)S(1)}, f32[512,256]{1,0:T(8,128)S(1)}, u32[]{:S(2)}, u32[]{:S(2)}) collective-permute-start(f32[512,256]{1,0:T(8,128)S(1)} %copy-done.1), channel_id=1, source_target_pairs={{0,1},{4,5},{8,11},{12,15},{16,19},{20,23},{24,26},{28,30}} | collective-permute-start | bytes 1572872 | tf_op jit(solution)/shard_map/ppermute | solution.py:406
  25.1 12.6 %collective-permute-start.12 = (f32[288,512]{1,0:T(8,128)S(1)}, f32[288,512]{1,0:T(8,128)S(1)}, u32[]{:S(2)}, u32[]{:S(2)}) collective-permute-start(f32[288,512]{1,0:T(8,128)S(1)} %broadcast_select_fusion), channel_id=1, source_target_pairs={{0,8},{1,9},{2,10},{3,11},{4,20},{5,21},{6,22},{7,23}} | collective-permute-start | bytes 1769480 | tf_op jit(solution)/shard_map/ppermute | solution.py:406
  26.4 12.6 %collective-permute-start.11 = (f32[288,512]{1,0:T(8,128)}, f32[288,512]{1,0:T(8,128)S(1)}, u32[]{:S(2)}, u32[]{:S(2)}) collective-permute-start(f32[288,512]{1,0:T(8,128)} %collective-permute-done.10), channel_id=1, source_target_pairs={{16,24},{17,25},{18,26},{19,27},{12,28},{13,29},{14,30},{15,31}} | collective-permute-start | bytes 1769480 | tf_op jit(solution)/shard_map/ppermute | solution.py:406
  33.7 7.4 %collective-permute-start.2 = (f32[128,384]{1,0:T(8,128)S(1)}, f32[128,384]{1,0:T(8,128)S(1)}, u32[]{:S(2)}, u32[]{:S(2)}) collective-permute-start(f32[128,384]{1,0:T(8,128)S(1)} %shard_map.42), channel_id=1, source_target_pairs={{0,24},{1,25},{2,26},{3,27}} | collective-permute-start | bytes 589832 | tf_op jit(solution)/shard_map/ppermute | solution.py:406
  36.0 5.2 %collective-permute-start.3 = (f32[128,384]{1,0:T(8,128)S(1)}, f32[128,384]{1,0:T(8,128)S(1)}, u32[]{:S(2)}, u32[]{:S(2)}) collective-permute-start(f32[128,384]{1,0:T(8,128)S(1)} %shard_map.42), channel_id=1, source_target_pairs={{0,16},{1,17},{2,18},{3,19}} | collective-permute-start | bytes 589832 | tf_op jit(solution)/shard_map/ppermute | solution.py:406
  37.7 4.5 %collective-permute-start.4 = (f32[128,384]{1,0:T(8,128)S(1)}, f32[128,384]{1,0:T(8,128)S(1)}, u32[]{:S(2)}, u32[]{:S(2)}) collective-permute-start(f32[128,384]{1,0:T(8,128)S(1)} %shard_map.42), channel_id=1, source_target_pairs={{0,8},{1,9},{2,10},{3,11}} | collective-permute-start | bytes 589832 | tf_op jit(solution)/shard_map/ppermute | solution.py:406
  39.0 5.8 %collective-permute-start.8 = (f32[512,256]{1,0:T(8,128)S(1)}, f32[512,256]{1,0:T(8,128)S(1)}, u32[]{:S(2)}, u32[]{:S(2)}) collective-permute-start(f32[512,256]{1,0:T(8,128)S(1)} %collective-permute-done.6.refs_1_), channel_id=1, source_target_pairs={{2,3},{6,7}} | collective-permute-start | bytes 1572872 | tf_op jit(solution)/shard_map/ppermute | solution.py:406
  41.1 3.9 %collective-permute-start.13 = (f32[288,512]{1,0:T(8,128)S(1)}, f32[288,512]{1,0:T(8,128)}, u32[]{:S(2)}, u32[]{:S(2)}) collective-permute-start(f32[288,512]{1,0:T(8,128)S(1)} %select_select_fusion.refs_4_.refs_3_), channel_id=1, source_target_pairs={{0,4},{4,0},{1,5},{5,1},{2,6},{6,2},{3,7},{7,3},{8,12},{12,8},{9,1... | collective-permute-start | bytes 1769480 | tf_op jit(solution)/shard_map/ppermute | solution.py:406
  42.2 2.8 %copy-start.2 = (f32[512,128]{1,0:T(8,128)S(1)}, f32[512,128]{1,0:T(8,128)}, u32[]{:S(2)}) copy-start(f32[512,128]{1,0:T(8,128)} %refs_2_.2) | copy-start | bytes 786436
  42.2 2.6 %collective-permute-start.5 = (f32[128,384]{1,0:T(8,128)S(1)}, f32[128,384]{1,0:T(8,128)S(1)}, u32[]{:S(2)}, u32[]{:S(2)}) collective-permute-start(f32[128,384]{1,0:T(8,128)S(1)} %select_select_fusion.1), channel_id=1, source_target_pairs={{0,4},{1,5},{2,6},{3,7},{8,12},{9,13},{10,14},{11,15},{16,20},{17,... | collective-permute-start | bytes 589832 | tf_op jit(solution)/shard_map/ppermute | solution.py:406
  44.9 10.3 %copy-start = (f32[512,1024]{1,0:T(8,128)S(1)}, f32[512,1024]{1,0:T(8,128)}, u32[]{:S(2)}) copy-start(f32[512,1024]{1,0:T(8,128)} %refs_2_.3) | copy-start | bytes 6291460
  47.4 12.2 %collective-permute-start.14 = (f32[128,128]{1,0:T(8,128)S(1)}, f32[128,128]{1,0:T(8,128)S(1)}, u32[]{:S(2)}, u32[]{:S(2)}) collective-permute-start(f32[128,128]{1,0:T(8,128)S(1)} %get-tuple-element.14), channel_id=1, source_target_pairs={{0,3},{1,2},{2,1},{3,0},{4,7},{5,6},{6,5},{7,4},{8,11},{9,10},{10,... | collective-permute-start | bytes 196616 | tf_op jit(solution)/shard_map/ppermute | solution.py:406
  54.6 5.2 %collective-permute-start.15 = (f32[128,128]{1,0:T(8,128)S(1)}, f32[128,128]{1,0:T(8,128)S(1)}, u32[]{:S(2)}, u32[]{:S(2)}) collective-permute-start(f32[128,128]{1,0:T(8,128)S(1)} %get-tuple-element.15), channel_id=1, source_target_pairs={{0,2},{1,3},{2,0},{3,1},{4,6},{5,7},{6,4},{7,5},{8,10},{9,11},{10,... | collective-permute-start | bytes 196616 | tf_op jit(solution)/shard_map/ppermute | solution.py:406
  54.6 5.2 %collective-permute-start.16 = (f32[128,128]{1,0:T(8,128)S(1)}, f32[128,128]{1,0:T(8,128)S(1)}, u32[]{:S(2)}, u32[]{:S(2)}) collective-permute-start(f32[128,128]{1,0:T(8,128)S(1)} %get-tuple-element.16), channel_id=1, source_target_pairs={{0,1},{1,0},{2,3},{3,2},{4,5},{5,4},{6,7},{7,6},{8,9},{9,8},{10,11... | collective-permute-start | bytes 196616 | tf_op jit(solution)/shard_map/ppermute | solution.py:406
where the time goes:
time: 61.2 us; the launch traced here: 60.6 us
  starting transfers between devices  34.3 us (56%)
  Pallas kernels  17.5 us (29%)
  other arithmetic  4.29 us (7%)
  waiting for transfers between devices  3.4 us (6%)
  between operations  1.03 us (2%)
    ppermute x17, starting transfers between devices, send(): return lax.ppermute(x, AXES, [(place(*a), place(*b)) for a, b in pairs])  34.3 us
    pallas_call x1, Pallas kernels, factor_inverse(): pl.pallas_call(factor_kernel, out_shape=jax.ShapeDtypeStruct(blocks.shape...  6.51 us
    pallas_call x1, Pallas kernels, trailing_update(): pl.pallas_call(lambda *refs: trailing_kernel(ratio, *refs), grid=(n // ta...  4.25 us
    ppermute x17, waiting for transfers between devices, send(): return lax.ppermute(x, AXES, [(place(*a), place(*b)) for a, b in pairs])  3.4 us
    pallas_call x1, Pallas kernels, payloads(): pl.pallas_call(lambda *refs: payload_kernel(ratio, *refs), in_specs=[IN_P...  2.67 us
    select_n x5, other arithmetic, choose(): out = jnp.where(index == i, options[i], out)  2.59 us
    pallas_call x1, Pallas kernels, solve_rows(): pl.pallas_call(lambda *refs: solve_kernel(col_size, ratio, *refs), grid=(...  2.38 us
    pallas_call x1, Pallas kernels, lead_blocks(): pl.pallas_call(lead_kernel, in_specs=[IN_PLACE], out_shape=jax.ShapeDtype...  1.6 us
  transfers between devices with their start and end apart: 17, of which 5 were waited for; matrix products, arithmetic and copies ran while one was open for 6% of the time, Pallas kernels for 21%

commit v1 on v0

--- a/solution.py
+++ b/solution.py
@@ -147,29 +147,7 @@
     out_ref[m:, :] = w_ref[:, m:]
 
 
-def lead_kernel(cov_ref, out_ref, sem):
-    copies = []
-    for i, (r, c) in enumerate(((0, 0), (1, 0), (1, 1))):
-        source = cov_ref.at[pl.ds(r * HALF, HALF), pl.ds(c * HALF, HALF)]
-        copies.append(pltpu.make_async_copy(source, out_ref.at[:, pl.ds(i * HALF, HALF)], sem.at[i]))
-    for copy in copies:
-        copy.start()
-    for copy in copies:
-        copy.wait()
-
-
-def lead_blocks(covariance):
-    return pl.pallas_call(
-        lead_kernel,
-        in_specs=[IN_PLACE],
-        out_shape=jax.ShapeDtypeStruct((HALF, 3 * HALF), jnp.float32),
-        scratch_shapes=[pltpu.SemaphoreType.DMA((3,))],
-        compiler_params=grant(63),
-        cost_estimate=pl.CostEstimate(flops=0, bytes_accessed=1 << 19, transcendentals=0),
-    )(covariance)
-
-
-def payload_kernel(ratio, cov_ref, pheno_ref, *refs):
+def cut_kernel(ratio, cov_ref, pheno_ref, lead_ref, *refs):
     out_refs, (rows_ref, head_ref, sem) = refs[:ratio], refs[ratio:]
     piece = out_refs[0].shape[1]
     copies = [
@@ -179,6 +157,10 @@
     for m in range(ratio):
         source = cov_ref.at[pl.ds(0, PANEL), pl.ds(m * piece, piece)]
         copies.append(pltpu.make_async_copy(source, out_refs[m].at[pl.ds(0, PANEL), :], sem.at[2 + m]))
+    for i, (r, c) in enumerate(((0, 0), (1, 0), (1, 1))):
+        source = cov_ref.at[pl.ds(r * HALF, HALF), pl.ds(c * HALF, HALF)]
+        target = lead_ref.at[:, pl.ds(i * HALF, HALF)]
+        copies.append(pltpu.make_async_copy(source, target, sem.at[2 + ratio + i]))
     for copy in copies:
         copy.start()
     copies[0].wait()
@@ -193,20 +175,44 @@
         copy.wait()
 
 
-def payloads(covariance, phenotypes, ratio):
+def cut(covariance, phenotypes, ratio):
     n, width = covariance.shape
     traits = phenotypes.shape[1]
     piece = width // ratio
     height = PANEL // ratio // (piece // traits)
     out = jax.ShapeDtypeStruct((PANEL + height, piece), jnp.float32)
     return pl.pallas_call(
-        lambda *refs: payload_kernel(ratio, *refs),
+        lambda *refs: cut_kernel(ratio, *refs),
         in_specs=[IN_PLACE] * 2,
-        out_shape=[out] * ratio + [jax.ShapeDtypeStruct((n, PANEL), jnp.float32)],
-        scratch_shapes=[pltpu.VMEM((PANEL, traits), jnp.float32), pltpu.SemaphoreType.DMA((2 + ratio,))],
-        compiler_params=grant(61.75),
+        out_shape=[jax.ShapeDtypeStruct((HALF, 3 * HALF), jnp.float32)]
+        + [out] * ratio
+        + [jax.ShapeDtypeStruct((n, PANEL), jnp.float32)],
+        scratch_shapes=[pltpu.VMEM((PANEL, traits), jnp.float32), pltpu.SemaphoreType.DMA((5 + ratio,))],
+        compiler_params=grant(61.9),
         cost_estimate=pl.CostEstimate(flops=0, bytes_accessed=4 * MIB, transcendentals=0),
     )(covariance, phenotypes)
+
+
+def pick_kernel(index_of, *refs):
+    options, out_ref = refs[:-1], refs[-1]
+    index = index_of(lax.axis_index("row"))
+    for i, option in enumerate(options):
+
+        @pl.when(index == i)
+        def _(option=option):
+            out_ref[...] = option[...]
+
+
+def pick(index_of, options):
+    shape = options[0].shape
+    return pl.pallas_call(
+        lambda *refs: pick_kernel(index_of, *refs),
+        in_specs=[pl.BlockSpec(memory_space=pltpu.VMEM)] * len(options),
+        out_specs=pl.BlockSpec(memory_space=pltpu.VMEM),
+        out_shape=jax.ShapeDtypeStruct(shape, jnp.float32),
+        compiler_params=grant(1 + (len(options) + 1) * options[0].size * 4 / MIB),
+        cost_estimate=pl.CostEstimate(flops=0, bytes_accessed=1 << 19, transcendentals=0),
+    )(*options)
 
 
 def rows_kernel(index_of, *refs):
@@ -397,7 +403,7 @@
     row_index, col_index = lax.axis_index("row"), lax.axis_index("col")
     ratio = row_size // col_size
     groups = row_size // ratio
-    group, member = row_index // ratio, lax.rem(row_index, ratio)
+    member = lax.rem(row_index, ratio)
 
     def place(r, c):
         return r * col_size + c
@@ -407,7 +413,7 @@
 
     every_group = [(k, c) for k in range(groups) for c in range(col_size)]
 
-    blocks = lead_blocks(covariance)
+    blocks, *pieces, own_rows = cut(covariance, phenotypes, ratio)
     found = []
     tree(list(range(col_size)), 1, {0: 0}, found)
     steps = {}
@@ -419,7 +425,6 @@
         new = [int(c in [d for _, d in steps[lv]]) for c in range(col_size)]
         diag = jnp.where(look_up(new, col_index) > 0, got, diag)
 
-    *pieces, own_rows = payloads(covariance, phenotypes, ratio)
     start = [pieces[0]]
     for m in range(1, ratio):
         start.append(send(pieces[m], [((0, c), (m, c)) for c in range(col_size)]))
@@ -464,7 +469,7 @@
     got = [inverse]
     for k in range(1, groups):
         got.append(send(inverse, [((0, c), (k * ratio, c)) for c in range(col_size)]))
-    inverse = choose(group, got)
+    inverse = pick(lambda row: row // ratio, got)
 
     arrived.append(send(arrived[0], [((r, relay_from), (r, col_size - 1)) for r in range(ratio)]))
     mine = choose(source, results)
@@ -492,7 +497,7 @@
     got = [inverse]
     for m in range(1, ratio):
         got.append(send(inverse, [((k * ratio, c), (k * ratio + m, c)) for k, c in every_group]))
-    inverse = choose(member, got)
+    inverse = pick(lambda row: lax.rem(row, ratio), got)
 
     panel, *parts = solve_rows(inverse, panel_raw, phenotypes, slabs, col_size)
     gathered = [parts[0]]

time: 61.2 us -> 62.4 us (1.020)
  waiting for transfers between devices: 3.4 us -> 7.78 us
  Pallas kernels: 17.5 us -> 16.1 us
  other arithmetic: 4.29 us -> 3.15 us
    ppermute x17, waiting for transfers between devices: 3.4 us -> 7.78 us  [send(): return lax.ppermute(x, AXES, [(place(*a), place(*b)) for a, b in pairs])]
    pallas_call x2 -> x3, Pallas kernels: 4.28 us -> 2.86 us  [the longest x1 2.82 us: cut(): pl.pallas_call(lambda *refs: cut_kernel(ratio, *refs), in_specs=[IN_PLACE...]
    select_n x5 -> x3, other arithmetic: 2.59 us -> 1.45 us  [choose(): out = jnp.where(index == i, options[i], out)]
  transfers between devices with their start and end apart: 17 -> 17, of which waited for: 5 -> 6; matrix products, arithmetic and copies ran while one was open for 6% -> 4% of each run, Pallas kernels for 21% -> 18%
where the time goes in v1:
time: 62.4 us; the launch traced here: 61.9 us
  starting transfers between devices  33.8 us (54%)
  Pallas kernels  16.1 us (26%)
  waiting for transfers between devices  7.78 us (12%)
  other arithmetic  3.15 us (5%)
  between operations  1.02 us (2%)
    ppermute x17, starting transfers between devices, send(): return lax.ppermute(x, AXES, [(place(*a), place(*b)) for a, b in pairs])  33.8 us
    ppermute x17, waiting for transfers between devices, send(): return lax.ppermute(x, AXES, [(place(*a), place(*b)) for a, b in pairs])  7.78 us
    pallas_call x1, Pallas kernels, factor_inverse(): pl.pallas_call(factor_kernel, out_shape=jax.ShapeDtypeStruct(blocks.shape...  6.51 us
    pallas_call x1, Pallas kernels, trailing_update(): pl.pallas_call(lambda *refs: trailing_kernel(ratio, *refs), grid=(n // ta...  4.25 us
    pallas_call x1, Pallas kernels, cut(): pl.pallas_call(lambda *refs: cut_kernel(ratio, *refs), in_specs=[IN_PLACE...  2.82 us
    pallas_call x1, Pallas kernels, solve_rows(): pl.pallas_call(lambda *refs: solve_kernel(col_size, ratio, *refs), grid=(...  2.38 us
    select_n x3, other arithmetic, choose(): out = jnp.where(index == i, options[i], out)  1.45 us
  transfers between devices with their start and end apart: 17, of which 6 were waited for; matrix products, arithmetic and copies ran while one was open for 4% of the time, Pallas kernels for 18%

profile of v1, /device:TPU:0, one launch (start us, length us, event | category | flops | bytes accessed | tf_op | source)
XLA Modules:
  0.0 61.9 jit_solution(14077173278246146428)
XLA Ops:
  0.6 2.8 %shard_map.41 = (f32[128,384]{1,0:T(8,128)}, f32[288,512]{1,0:T(8,128)}, f32[288,512]{1,0:T(8,128)}, f32[512,256]{1,0:T(8,128)}) custom-call(f32[512,1024]{1,0:T(8,128)} %refs_2_.3, f32[512,128]{1,0:T(8,128)} %refs_2_.2), custom_call_target="tpu_custom_call" | custom-call | bytes 4194304 | tf_op jit(solution)/shard_map/pallas_call | solution.py:184
  3.5 0.0 copy-start.1
  3.5 2.6 %collective-permute-start.9 = (f32[288,512]{1,0:T(8,128)}, f32[288,512]{1,0:T(8,128)S(1)}, u32[]{:S(2)}, u32[]{:S(2)}) collective-permute-start(f32[288,512]{1,0:T(8,128)} %get-tuple-element.13), channel_id=1, source_target_pairs={{0,4},{1,5},{2,6},{3,7}} | collective-permute-start | bytes 1769480 | tf_op jit(solution)/shard_map/ppermute | solution.py:412
  6.0 5.3 %collective-permute-start = (f32[128,384]{1,0:T(8,128)}, f32[128,384]{1,0:T(8,128)S(1)}, u32[]{:S(2)}, u32[]{:S(2)}) collective-permute-start(f32[128,384]{1,0:T(8,128)} %get-tuple-element.11), channel_id=1, source_target_pairs={{0,2}} | collective-permute-start | bytes 589832 | tf_op jit(solution)/shard_map/ppermute | solution.py:412
  11.4 0.0 collective-permute-done.9
  11.4 1.2 %broadcast_select_fusion = f32[288,512]{1,0:T(8,128)S(1)} fusion(f32[288,512]{1,0:T(8,128)S(1)} %collective-permute-done.9, f32[288,512]{1,0:T(8,128)} %get-tuple-element.14, pred[]{:T(512)S(6)} %eq.79), kind=kLoop, calls=%fused_computation.1 | loop fusion | flops 147456 | bytes 1769473 | tf_op jit(solution)/shard_map/jit(_where)/select_n | solution.py:389
  12.6 1.3 %collective-permute-start.10 = (f32[288,512]{1,0:T(8,128)S(1)}, f32[288,512]{1,0:T(8,128)S(1)}, u32[]{:S(2)}, u32[]{:S(2)}) collective-permute-start(f32[288,512]{1,0:T(8,128)S(1)} %broadcast_select_fusion), channel_id=1, source_target_pairs={{0,16},{1,17},{2,18},{3,19},{4,12},{5,13},{6,14},{7,15}} | collective-permute-start | bytes 1769480 | tf_op jit(solution)/shard_map/ppermute | solution.py:412
  13.9 0.9 %collective-permute-done = f32[128,384]{1,0:T(8,128)S(1)} collective-permute-done((f32[128,384]{1,0:T(8,128)}, f32[128,384]{1,0:T(8,128)S(1)}, u32[]{:S(2)}, u32[]{:S(2)}) %collective-permute-start) | collective-permute-done | bytes 196640 | tf_op jit(solution)/shard_map/ppermute | solution.py:412
  14.8 0.9 %broadcast_select_fusion.1 = f32[128,384]{1,0:T(8,128)S(1)} fusion(f32[128,384]{1,0:T(8,128)S(1)} %collective-permute-done, f32[128,384]{1,0:T(8,128)} %get-tuple-element.11, pred[]{:T(512)S(6)} %gt.7), kind=kLoop, calls=%fused_computation.3 | loop fusion | flops 49152 | bytes 589825 | tf_op jit(solution)/shard_map/jit(_where)/select_n | solution.py:426
  15.8 1.3 %collective-permute-start.1 = (f32[128,384]{1,0:T(8,128)S(1)}, f32[128,384]{1,0:T(8,128)S(1)}, u32[]{:S(2)}, u32[]{:S(2)}) collective-permute-start(f32[128,384]{1,0:T(8,128)S(1)} %broadcast_select_fusion.1), channel_id=1, source_target_pairs={{0,1},{2,3}} | collective-permute-start | bytes 589832 | tf_op jit(solution)/shard_map/ppermute | solution.py:412
  17.1 0.0 copy-done.1
  17.1 4.3 %collective-permute-start.6 = (f32[512,256]{1,0:T(8,128)S(1)}, f32[512,256]{1,0:T(8,128)S(1)}, u32[]{:S(2)}, u32[]{:S(2)}) collective-permute-start(f32[512,256]{1,0:T(8,128)S(1)} %copy-done.1), channel_id=1, source_target_pairs={{0,2},{4,6},{8,10},{12,14},{16,17},{20,21},{24,25},{28,29}} | collective-permute-start | bytes 1572872 | tf_op jit(solution)/shard_map/ppermute | solution.py:412
  21.5 1.3 %collective-permute-start.12 = (f32[288,512]{1,0:T(8,128)S(1)}, f32[288,512]{1,0:T(8,128)S(1)}, u32[]{:S(2)}, u32[]{:S(2)}) collective-permute-start(f32[288,512]{1,0:T(8,128)S(1)} %broadcast_select_fusion), channel_id=1, source_target_pairs={{0,8},{1,9},{2,10},{3,11},{4,20},{5,21},{6,22},{7,23}} | collective-permute-start | bytes 1769480 | tf_op jit(solution)/shard_map/ppermute | solution.py:412
  22.8 2.3 %collective-permute-done.10 = f32[288,512]{1,0:T(8,128)S(1)} collective-permute-done((f32[288,512]{1,0:T(8,128)S(1)}, f32[288,512]{1,0:T(8,128)S(1)}, u32[]{:S(2)}, u32[]{:S(2)}) %collective-permute-start.10) | collective-permute-done | bytes 589856 | tf_op jit(solution)/shard_map/ppermute | solution.py:412
  25.1 0.7 %collective-permute-start.11 = (f32[288,512]{1,0:T(8,128)S(1)}, f32[288,512]{1,0:T(8,128)S(1)}, u32[]{:S(2)}, u32[]{:S(2)}) collective-permute-start(f32[288,512]{1,0:T(8,128)S(1)} %collective-permute-done.10), channel_id=1, source_target_pairs={{16,24},{17,25},{18,26},{19,27},{12,28},{13,29},{14,30},{15,31}} | collective-permute-start | bytes 1769480 | tf_op jit(solution)/shard_map/ppermute | solution.py:412
  25.8 0.0 collective-permute-done.1
  25.8 6.5 %shard_map.42.refs_0_ = f32[128,384]{1,0:T(8,128)S(1)} custom-call(f32[128,384]{1,0:T(8,128)S(1)} %broadcast_select_fusion.2.d_ref), custom_call_target="tpu_custom_call" | custom-call | flops 4294967296 | bytes 524288 | tf_op jit(solution)/shard_map/pallas_call | solution.py:134
  32.4 1.3 %collective-permute-start.2 = (f32[128,384]{1,0:T(8,128)S(1)}, f32[128,384]{1,0:T(8,128)S(1)}, u32[]{:S(2)}, u32[]{:S(2)}) collective-permute-start(f32[128,384]{1,0:T(8,128)S(1)} %shard_map.42.refs_0_), channel_id=1, source_target_pairs={{0,8},{1,9},{2,10},{3,11}} | collective-permute-start | bytes 589832 | tf_op jit(solution)/shard_map/ppermute | solution.py:412
  33.7 0.0 collective-permute-done.12
  33.7 0.0 collective-permute-done.11
  33.7 0.3 select_select_fusion.refs_4_.refs_3_
  34.0 0.1 collective-permute-start.13
  34.0 1.3 %collective-permute-start.7 = (f32[512,256]{1,0:T(8,128)S(1)}, f32[512,256]{1,0:T(8,128)S(1)}, u32[]{:S(2)}, u32[]{:S(2)}) collective-permute-start(f32[512,256]{1,0:T(8,128)S(1)} %copy-done.1), channel_id=1, source_target_pairs={{0,1},{4,5},{8,11},{12,15},{16,19},{20,23},{24,26},{28,30}} | collective-permute-start | bytes 1572872 | tf_op jit(solution)/shard_map/ppermute | solution.py:412
  35.4 0.0 collective-permute-done.6.refs_1_
  35.4 0.7 %collective-permute-start.8 = (f32[512,256]{1,0:T(8,128)S(1)}, f32[512,256]{1,0:T(8,128)S(1)}, u32[]{:S(2)}, u32[]{:S(2)}) collective-permute-start(f32[512,256]{1,0:T(8,128)S(1)} %collective-permute-done.6.refs_1_), channel_id=1, source_target_pairs={{2,3},{6,7}} | collective-permute-start | bytes 1572872 | tf_op jit(solution)/shard_map/ppermute | solution.py:412
  36.1 5.8 %collective-permute-start.3 = (f32[128,384]{1,0:T(8,128)S(1)}, f32[128,384]{1,0:T(8,128)S(1)}, u32[]{:S(2)}, u32[]{:S(2)}) collective-permute-start(f32[128,384]{1,0:T(8,128)S(1)} %shard_map.42.refs_0_), channel_id=1, source_target_pairs={{0,16},{1,17},{2,18},{3,19}} | collective-permute-start | bytes 589832 | tf_op jit(solution)/shard_map/ppermute | solution.py:412
  41.9 0.0 collective-permute-done.2.refs_1_
  41.9 1.9 %collective-permute-start.4 = (f32[128,384]{1,0:T(8,128)S(1)}, f32[128,384]{1,0:T(8,128)S(1)}, u32[]{:S(2)}, u32[]{:S(2)}) collective-permute-start(f32[128,384]{1,0:T(8,128)S(1)} %shard_map.42.refs_0_), channel_id=1, source_target_pairs={{0,24},{1,25},{2,26},{3,27}} | collective-permute-start | bytes 589832 | tf_op jit(solution)/shard_map/ppermute | solution.py:412
  43.8 1.2 %collective-permute-done.3.refs_2_ = f32[128,384]{1,0:T(8,128)S(1)} collective-permute-done((f32[128,384]{1,0:T(8,128)S(1)}, f32[128,384]{1,0:T(8,128)S(1)}, u32[]{:S(2)}, u32[]{:S(2)}) %collective-permute-start.3) | collective-permute-done | bytes 196640 | tf_op jit(solution)/shard_map/ppermute | solution.py:412
  45.1 1.9 %collective-permute-done.4.refs_3_ = f32[128,384]{1,0:T(8,128)S(1)} collective-permute-done((f32[128,384]{1,0:T(8,128)S(1)}, f32[128,384]{1,0:T(8,128)S(1)}, u32[]{:S(2)}, u32[]{:S(2)}) %collective-permute-start.4) | collective-permute-done | bytes 196640 | tf_op jit(solution)/shard_map/ppermute | solution.py:412
  47.0 0.0 copy-start.2
  47.0 1.4 %collective-permute-start.5 = (f32[128,384]{1,0:T(8,128)S(1)}, f32[128,384]{1,0:T(8,128)S(1)}, u32[]{:S(2)}, u32[]{:S(2)}) collective-permute-start(f32[128,384]{1,0:T(8,128)S(1)} %shard_map.43.refs_0_), channel_id=1, source_target_pairs={{0,4},{1,5},{2,6},{3,7},{8,12},{9,13},{10,14},{11,15},{16,20},{17,... | collective-permute-start | bytes 589832 | tf_op jit(solution)/shard_map/ppermute | solution.py:412
  48.5 1.0 %collective-permute-done.5.refs_1_ = f32[128,384]{1,0:T(8,128)S(1)} collective-permute-done((f32[128,384]{1,0:T(8,128)S(1)}, f32[128,384]{1,0:T(8,128)S(1)}, u32[]{:S(2)}, u32[]{:S(2)}) %collective-permute-start.5) | collective-permute-done | bytes 196640 | tf_op jit(solution)/shard_map/ppermute | solution.py:412
  49.5 0.0 collective-permute-done.7.refs_2_
  49.5 0.0 collective-permute-done.8.refs_3_
  49.5 0.1 shard_map.45.refs_1_
  49.6 0.0 copy-start
  49.7 0.0 collective-permute-done.13.refs_4_
  49.7 0.0 copy-done.2
  49.7 2.4 %shard_map.46 = (f32[512,256]{1,0:T(8,128)S(1)}, f32[128,128]{1,0:T(8,128)S(1)}, f32[128,128]{1,0:T(8,128)S(1)}, f32[128,128]{1,0:T(8,128)S(1)}, f32[128,128]{1,0:T(8,128)S(1)}) custom-call(f32[128,384]{1,0:T(8,128)S(1)} %shard_map.44.refs_0_, f32[512,256]{1,0:T(8,128)S(1)} %shard_map.45.refs_1_, f32[512,128]{1,0:T(8,128)S(1)} %copy-done.2, ...), custom_call_target="tpu_custom_call" | custom-call | flops 1073741824 | bytes 2097152 | tf_op jit(solution)/shard_map/pallas_call | solution.py:297
  52.1 2.2 %collective-permute-start.14 = (f32[128,128]{1,0:T(8,128)S(1)}, f32[128,128]{1,0:T(8,128)S(1)}, u32[]{:S(2)}, u32[]{:S(2)}) collective-permute-start(f32[128,128]{1,0:T(8,128)S(1)} %get-tuple-element.16), channel_id=1, source_target_pairs={{0,3},{1,2},{2,1},{3,0},{4,7},{5,6},{6,5},{7,4},{8,11},{9,10},{10,... | collective-permute-start | bytes 196616 | tf_op jit(solution)/shard_map/ppermute | solution.py:412
  54.2 0.0 collective-permute-start.15
  54.2 2.3 %collective-permute-start.16 = (f32[128,128]{1,0:T(8,128)S(1)}, f32[128,128]{1,0:T(8,128)S(1)}, u32[]{:S(2)}, u32[]{:S(2)}) collective-permute-start(f32[128,128]{1,0:T(8,128)S(1)} %get-tuple-element.18), channel_id=1, source_target_pairs={{0,1},{1,0},{2,3},{3,2},{4,5},{5,4},{6,7},{7,6},{8,9},{9,8},{10,11... | collective-permute-start | bytes 196616 | tf_op jit(solution)/shard_map/ppermute | solution.py:412
  56.5 0.0 copy-done
  56.5 4.2 %shard_map.47 = f32[512,1024]{1,0:T(8,128)} custom-call(f32[128,384]{1,0:T(8,128)S(1)} %shard_map.44.refs_0_, f32[512,256]{1,0:T(8,128)S(1)} %get-tuple-element.15.refs_1_, f32[512,1024]{1,0:T(8,128)S(1)} %copy-done, f32[288,512]{1,0:T(8,128)S(1)} %select_select_fusion.refs_4_.refs_3_, f32[288,512]{1,0:T(8,128)} %collective-permute-done.13.refs_4_), custom_call_target="tpu_custom_call" | custom-call | flops 2147483648 | bytes 6291456 | tf_op jit(solution)/shard_map/pallas_call | solution.py:349
  60.8 0.0 collective-permute-done.14
  60.8 0.3 collective-permute-done.15
  61.1 0.0 collective-permute-done.16
  61.1 0.7 %pad_maximum_fusion = f32[128,512]{1,0:T(8,128)} fusion(f32[128,128]{1,0:T(8,128)S(1)} %get-tuple-element.21, f32[128,128]{1,0:T(8,128)S(1)} %get-tuple-element.22, f32[128,128]{1,0:T(8,128)S(1)} %get-tuple-element.23, f32[128,128]{1,0:T(8,128)S(1)} %get-tuple-element.20), kind=kLoop, calls=%fused_computation.2 | loop fusion | flops 196608 | bytes 524288 | tf_op jit(solution)/shard_map/concatenate | solution.py:508
  (4 shorter events, 0.1 us)
Async XLA Ops:
  3.5 13.7 %copy-start.1 = (f32[512,256]{1,0:T(8,128)S(1)}, f32[512,256]{1,0:T(8,128)}, u32[]{:S(2)}) copy-start(f32[512,256]{1,0:T(8,128)} %get-tuple-element.12.refs_0_) | copy-start | bytes 1572868
  3.5 7.9 %collective-permute-start.9 = (f32[288,512]{1,0:T(8,128)}, f32[288,512]{1,0:T(8,128)S(1)}, u32[]{:S(2)}, u32[]{:S(2)}) collective-permute-start(f32[288,512]{1,0:T(8,128)} %get-tuple-element.13), channel_id=1, source_target_pairs={{0,4},{1,5},{2,6},{3,7}} | collective-permute-start | bytes 1769480 | tf_op jit(solution)/shard_map/ppermute | solution.py:412
  6.0 8.8 %collective-permute-start = (f32[128,384]{1,0:T(8,128)}, f32[128,384]{1,0:T(8,128)S(1)}, u32[]{:S(2)}, u32[]{:S(2)}) collective-permute-start(f32[128,384]{1,0:T(8,128)} %get-tuple-element.11), channel_id=1, source_target_pairs={{0,2}} | collective-permute-start | bytes 589832 | tf_op jit(solution)/shard_map/ppermute | solution.py:412
  12.6 12.5 %collective-permute-start.10 = (f32[288,512]{1,0:T(8,128)S(1)}, f32[288,512]{1,0:T(8,128)S(1)}, u32[]{:S(2)}, u32[]{:S(2)}) collective-permute-start(f32[288,512]{1,0:T(8,128)S(1)} %broadcast_select_fusion), channel_id=1, source_target_pairs={{0,16},{1,17},{2,18},{3,19},{4,12},{5,13},{6,14},{7,15}} | collective-permute-start | bytes 1769480 | tf_op jit(solution)/shard_map/ppermute | solution.py:412
  15.8 10.0 %collective-permute-start.1 = (f32[128,384]{1,0:T(8,128)S(1)}, f32[128,384]{1,0:T(8,128)S(1)}, u32[]{:S(2)}, u32[]{:S(2)}) collective-permute-start(f32[128,384]{1,0:T(8,128)S(1)} %broadcast_select_fusion.1), channel_id=1, source_target_pairs={{0,1},{2,3}} | collective-permute-start | bytes 589832 | tf_op jit(solution)/shard_map/ppermute | solution.py:412
  17.1 18.3 %collective-permute-start.6 = (f32[512,256]{1,0:T(8,128)S(1)}, f32[512,256]{1,0:T(8,128)S(1)}, u32[]{:S(2)}, u32[]{:S(2)}) collective-permute-start(f32[512,256]{1,0:T(8,128)S(1)} %copy-done.1), channel_id=1, source_target_pairs={{0,2},{4,6},{8,10},{12,14},{16,17},{20,21},{24,25},{28,29}} | collective-permute-start | bytes 1572872 | tf_op jit(solution)/shard_map/ppermute | solution.py:412
  21.5 12.2 %collective-permute-start.12 = (f32[288,512]{1,0:T(8,128)S(1)}, f32[288,512]{1,0:T(8,128)S(1)}, u32[]{:S(2)}, u32[]{:S(2)}) collective-permute-start(f32[288,512]{1,0:T(8,128)S(1)} %broadcast_select_fusion), channel_id=1, source_target_pairs={{0,8},{1,9},{2,10},{3,11},{4,20},{5,21},{6,22},{7,23}} | collective-permute-start | bytes 1769480 | tf_op jit(solution)/shard_map/ppermute | solution.py:412
  25.1 8.6 %collective-permute-start.11 = (f32[288,512]{1,0:T(8,128)S(1)}, f32[288,512]{1,0:T(8,128)S(1)}, u32[]{:S(2)}, u32[]{:S(2)}) collective-permute-start(f32[288,512]{1,0:T(8,128)S(1)} %collective-permute-done.10), channel_id=1, source_target_pairs={{16,24},{17,25},{18,26},{19,27},{12,28},{13,29},{14,30},{15,31}} | collective-permute-start | bytes 1769480 | tf_op jit(solution)/shard_map/ppermute | solution.py:412
  32.4 9.5 %collective-permute-start.2 = (f32[128,384]{1,0:T(8,128)S(1)}, f32[128,384]{1,0:T(8,128)S(1)}, u32[]{:S(2)}, u32[]{:S(2)}) collective-permute-start(f32[128,384]{1,0:T(8,128)S(1)} %shard_map.42.refs_0_), channel_id=1, source_target_pairs={{0,8},{1,9},{2,10},{3,11}} | collective-permute-start | bytes 589832 | tf_op jit(solution)/shard_map/ppermute | solution.py:412
  34.0 15.7 %collective-permute-start.13 = (f32[288,512]{1,0:T(8,128)S(1)}, f32[288,512]{1,0:T(8,128)}, u32[]{:S(2)}, u32[]{:S(2)}) collective-permute-start(f32[288,512]{1,0:T(8,128)S(1)} %select_select_fusion.refs_4_.refs_3_), channel_id=1, source_target_pairs={{0,4},{4,0},{1,5},{5,1},{2,6},{6,2},{3,7},{7,3},{8,12},{12,8},{9,1... | collective-permute-start | bytes 1769480 | tf_op jit(solution)/shard_map/ppermute | solution.py:412
  34.0 15.5 %collective-permute-start.7 = (f32[512,256]{1,0:T(8,128)S(1)}, f32[512,256]{1,0:T(8,128)S(1)}, u32[]{:S(2)}, u32[]{:S(2)}) collective-permute-start(f32[512,256]{1,0:T(8,128)S(1)} %copy-done.1), channel_id=1, source_target_pairs={{0,1},{4,5},{8,11},{12,15},{16,19},{20,23},{24,26},{28,30}} | collective-permute-start | bytes 1572872 | tf_op jit(solution)/shard_map/ppermute | solution.py:412
  35.4 14.2 %collective-permute-start.8 = (f32[512,256]{1,0:T(8,128)S(1)}, f32[512,256]{1,0:T(8,128)S(1)}, u32[]{:S(2)}, u32[]{:S(2)}) collective-permute-start(f32[512,256]{1,0:T(8,128)S(1)} %collective-permute-done.6.refs_1_), channel_id=1, source_target_pairs={{2,3},{6,7}} | collective-permute-start | bytes 1572872 | tf_op jit(solution)/shard_map/ppermute | solution.py:412
  36.1 9.0 %collective-permute-start.3 = (f32[128,384]{1,0:T(8,128)S(1)}, f32[128,384]{1,0:T(8,128)S(1)}, u32[]{:S(2)}, u32[]{:S(2)}) collective-permute-start(f32[128,384]{1,0:T(8,128)S(1)} %shard_map.42.refs_0_), channel_id=1, source_target_pairs={{0,16},{1,17},{2,18},{3,19}} | collective-permute-start | bytes 589832 | tf_op jit(solution)/shard_map/ppermute | solution.py:412
  41.9 5.1 %collective-permute-start.4 = (f32[128,384]{1,0:T(8,128)S(1)}, f32[128,384]{1,0:T(8,128)S(1)}, u32[]{:S(2)}, u32[]{:S(2)}) collective-permute-start(f32[128,384]{1,0:T(8,128)S(1)} %shard_map.42.refs_0_), channel_id=1, source_target_pairs={{0,24},{1,25},{2,26},{3,27}} | collective-permute-start | bytes 589832 | tf_op jit(solution)/shard_map/ppermute | solution.py:412
  47.0 2.7 %copy-start.2 = (f32[512,128]{1,0:T(8,128)S(1)}, f32[512,128]{1,0:T(8,128)}, u32[]{:S(2)}) copy-start(f32[512,128]{1,0:T(8,128)} %refs_2_.2) | copy-start | bytes 786436
  47.0 2.5 %collective-permute-start.5 = (f32[128,384]{1,0:T(8,128)S(1)}, f32[128,384]{1,0:T(8,128)S(1)}, u32[]{:S(2)}, u32[]{:S(2)}) collective-permute-start(f32[128,384]{1,0:T(8,128)S(1)} %shard_map.43.refs_0_), channel_id=1, source_target_pairs={{0,4},{1,5},{2,6},{3,7},{8,12},{9,13},{10,14},{11,15},{16,20},{17,... | collective-permute-start | bytes 589832 | tf_op jit(solution)/shard_map/ppermute | solution.py:412
  49.6 6.9 %copy-start = (f32[512,1024]{1,0:T(8,128)S(1)}, f32[512,1024]{1,0:T(8,128)}, u32[]{:S(2)}) copy-start(f32[512,1024]{1,0:T(8,128)} %refs_2_.3) | copy-start | bytes 6291460
  52.1 8.7 %collective-permute-start.14 = (f32[128,128]{1,0:T(8,128)S(1)}, f32[128,128]{1,0:T(8,128)S(1)}, u32[]{:S(2)}, u32[]{:S(2)}) collective-permute-start(f32[128,128]{1,0:T(8,128)S(1)} %get-tuple-element.16), channel_id=1, source_target_pairs={{0,3},{1,2},{2,1},{3,0},{4,7},{5,6},{6,5},{7,4},{8,11},{9,10},{10,... | collective-permute-start | bytes 196616 | tf_op jit(solution)/shard_map/ppermute | solution.py:412
  54.2 6.9 %collective-permute-start.15 = (f32[128,128]{1,0:T(8,128)S(1)}, f32[128,128]{1,0:T(8,128)S(1)}, u32[]{:S(2)}, u32[]{:S(2)}) collective-permute-start(f32[128,128]{1,0:T(8,128)S(1)} %get-tuple-element.17), channel_id=1, source_target_pairs={{0,2},{1,3},{2,0},{3,1},{4,6},{5,7},{6,4},{7,5},{8,10},{9,11},{10,... | collective-permute-start | bytes 196616 | tf_op jit(solution)/shard_map/ppermute | solution.py:412
  54.2 6.9 %collective-permute-start.16 = (f32[128,128]{1,0:T(8,128)S(1)}, f32[128,128]{1,0:T(8,128)S(1)}, u32[]{:S(2)}, u32[]{:S(2)}) collective-permute-start(f32[128,128]{1,0:T(8,128)S(1)} %get-tuple-element.18), channel_id=1, source_target_pairs={{0,1},{1,0},{2,3},{3,2},{4,5},{5,4},{6,7},{7,6},{8,9},{9,8},{10,11... | collective-permute-start | bytes 196616 | tf_op jit(solution)/shard_map/ppermute | solution.py:412

commit v2 on v1

--- a/solution.py
+++ b/solution.py
@@ -115,7 +115,9 @@
                 t[h] = acc
 
 
-def factor_kernel(d_ref, w_ref, w11_ref, w22_ref):
+def factor_kernel(*refs):
+    options, (w_ref, d_ref, w11_ref, w22_ref, sem) = refs[:-5], refs[-5:]
+    fetch(lax.axis_index("col"), options, d_ref, sem)
     m = d_ref.shape[0]
     eliminate(d_ref[:, :m], w11_ref)
     w11 = w11_ref[...]
@@ -129,15 +131,17 @@
     w_ref[:, 2 * m :] = w22
 
 
-def factor_inverse(blocks):
-    m = blocks.shape[0]
+def factor_inverse(options):
+    shape = options[0].shape
+    square = pltpu.VMEM((shape[0], shape[0]), jnp.float32)
     return pl.pallas_call(
         factor_kernel,
-        out_shape=jax.ShapeDtypeStruct(blocks.shape, jnp.float32),
-        scratch_shapes=[pltpu.VMEM((m, m), jnp.float32)] * 2,
+        in_specs=[ANYWHERE] * len(options),
+        out_shape=jax.ShapeDtypeStruct(shape, jnp.float32),
+        scratch_shapes=[pltpu.VMEM(shape, jnp.float32), square, square, pltpu.SemaphoreType.DMA(())],
         compiler_params=grant(4),
         cost_estimate=pl.CostEstimate(flops=1 << 32, bytes_accessed=1 << 19, transcendentals=0),
-    )(blocks)
+    )(*options)
 
 
 def full_inverse(w_ref, out_ref):
@@ -215,9 +219,7 @@
     )(*options)
 
 
-def rows_kernel(index_of, *refs):
-    options, slab_ref, out_ref, sem = refs[:-3], refs[-3], refs[-2], refs[-1]
-    index = index_of(lax.axis_index("row"), lax.axis_index("col"))
+def fetch(index, options, out_ref, sem):
     for i, option in enumerate(options):
 
         @pl.when(index == i)
@@ -225,6 +227,29 @@
             copy = pltpu.make_async_copy(option, out_ref, sem)
             copy.start()
             copy.wait()
+
+
+def fetch_kernel(index_of, *refs):
+    fetch(index_of(lax.axis_index("row")), refs[:-2], refs[-2], refs[-1])
+
+
+def pick_large(index_of, options):
+    shape = options[0].shape
+    return pl.pallas_call(
+        lambda *refs: fetch_kernel(index_of, *refs),
+        in_specs=[ANYWHERE] * len(options),
+        out_specs=pl.BlockSpec(memory_space=pltpu.VMEM),
+        out_shape=jax.ShapeDtypeStruct(shape, jnp.float32),
+        scratch_shapes=[pltpu.SemaphoreType.DMA(())],
+        compiler_params=grant(4),
+        cost_estimate=pl.CostEstimate(flops=0, bytes_accessed=MIB, transcendentals=0),
+    )(*options)
+
+
+def rows_kernel(index_of, *refs):
+    options, slab_ref, out_ref, sem = refs[:-3], refs[-3], refs[-2], refs[-1]
+    index = index_of(lax.axis_index("row"), lax.axis_index("col"))
+    fetch(index, options, out_ref, sem)
 
     @pl.when(index == len(options))
     def _():
@@ -414,21 +439,14 @@
     every_group = [(k, c) for k in range(groups) for c in range(col_size)]
 
     blocks, *pieces, own_rows = cut(covariance, phenotypes, ratio)
-    found = []
-    tree(list(range(col_size)), 1, {0: 0}, found)
-    steps = {}
-    for lv, sl, s, d in found:
-        steps.setdefault(lv, []).append((s, d))
-    diag = blocks
-    for lv in sorted(steps):
-        got = send(diag, [((0, s), (0, d)) for s, d in steps[lv]])
-        new = [int(c in [d for _, d in steps[lv]]) for c in range(col_size)]
-        diag = jnp.where(look_up(new, col_index) > 0, got, diag)
+    diag = [blocks]
+    for c in range(1, col_size):
+        diag.append(send(blocks, [((0, 0), (0, c))]))
 
     start = [pieces[0]]
     for m in range(1, ratio):
         start.append(send(pieces[m], [((0, c), (m, c)) for c in range(col_size)]))
-    start = choose(row_index, start)
+    start = pick_large(lambda row: jnp.minimum(row, ratio - 1), start)
     stages = {}
     came = {}
     for m in range(ratio):
@@ -450,7 +468,7 @@
             held[key[0]] = jnp.where(look_up(here, row_index) > 0, got, held[key[0]])
         else:
             held[key[0]] = got
-    source = look_up([keys.index(came[r]) + 1 if r in came else 0 for r in range(row_size)], row_index)
+    source = [keys.index(came[r]) + 1 if r in came else 0 for r in range(row_size)]
 
     relay_from = col_size // 2
     targets = []
@@ -472,7 +490,7 @@
     inverse = pick(lambda row: row // ratio, got)
 
     arrived.append(send(arrived[0], [((r, relay_from), (r, col_size - 1)) for r in range(ratio)]))
-    mine = choose(source, results)
+    mine = pick_large(lambda row: look_up(source, row), results)
     slabs = [mine]
     for s in range(1, ratio):
         slabs.append(

time: 62.4 us -> 63.6 us (1.019)
  other arithmetic: 3.15 us -> 0.76 us
  local copies, waits for them, and re-layouts: 0.02 us -> 2 us
  waiting for transfers between devices: 7.78 us -> 8.61 us
    unnamed x6 -> x10, local copies, waits for them, and re-layouts: 0.02 us -> 2 us
    select_n x3 -> x1, other arithmetic: 1.45 us -> 0.03 us  [choose(): out = jnp.where(index == i, options[i], out)]
    select_n x2 -> x0, other arithmetic: 0.97 us -> none  [shards(): diag = jnp.where(look_up(new, col_index) > 0, got, diag)]
    ppermute x17 -> x18, waiting for transfers between devices: 7.78 us -> 8.61 us  [send(): return lax.ppermute(x, AXES, [(place(*a), place(*b)) for a, b in pairs])]
    pallas_call x1 -> x3, Pallas kernels: 6.51 us -> 7.06 us  [the longest x1 6.76 us: factor_inverse(): pl.pallas_call(factor_kernel, in_specs=[ANYWHERE] * len(options), out_sha...]
    ppermute x17 -> x18, starting transfers between devices: 33.8 us -> 34.1 us  [send(): return lax.ppermute(x, AXES, [(place(*a), place(*b)) for a, b in pairs])]
  transfers between devices with their start and end apart: 17 -> 18, of which waited for: 6 -> 6; matrix products, arithmetic and copies ran while one was open for 4% -> 0% of each run, Pallas kernels for 18% -> 18%
where the time goes in v2:
time: 63.6 us; the launch traced here: 63.1 us
  starting transfers between devices  34.1 us (54%)
  Pallas kernels  16.7 us (26%)
  waiting for transfers between devices  8.61 us (14%)
  local copies, waits for them, and re-layouts  2 us (3%)
  between operations  0.98 us (2%)
  other arithmetic  0.76 us (1%)
    ppermute x18, starting transfers between devices, send(): return lax.ppermute(x, AXES, [(place(*a), place(*b)) for a, b in pairs])  34.1 us
    ppermute x18, waiting for transfers between devices, send(): return lax.ppermute(x, AXES, [(place(*a), place(*b)) for a, b in pairs])  8.61 us
    pallas_call x1, Pallas kernels, factor_inverse(): pl.pallas_call(factor_kernel, in_specs=[ANYWHERE] * len(options), out_sha...  6.76 us
    pallas_call x1, Pallas kernels, trailing_update(): pl.pallas_call(lambda *refs: trailing_kernel(ratio, *refs), grid=(n // ta...  4.25 us
    pallas_call x1, Pallas kernels, cut(): pl.pallas_call(lambda *refs: cut_kernel(ratio, *refs), in_specs=[IN_PLACE...  2.83 us
    pallas_call x1, Pallas kernels, solve_rows(): pl.pallas_call(lambda *refs: solve_kernel(col_size, ratio, *refs), grid=(...  2.38 us
    unnamed x10, local copies, waits for them, and re-layouts  2 us
  transfers between devices with their start and end apart: 18, of which 6 were waited for; matrix products, arithmetic and copies ran while one was open for 0% of the time, Pallas kernels for 18%

profile of v2, /device:TPU:0, one launch (start us, length us, event | category | flops | bytes accessed | tf_op | source)
XLA Modules:
  0.0 63.1 jit_solution(15755707590729597903)
XLA Ops:
  0.6 2.8 %shard_map.41 = (f32[128,384]{1,0:T(8,128)}, f32[288,512]{1,0:T(8,128)}, f32[288,512]{1,0:T(8,128)}, f32[512,256]{1,0:T(8,128)}) custom-call(f32[512,1024]{1,0:T(8,128)} %refs_2_.3, f32[512,128]{1,0:T(8,128)} %refs_2_.2), custom_call_target="tpu_custom_call" | custom-call | bytes 4194304 | tf_op jit(solution)/shard_map/pallas_call | solution.py:188
  3.5 2.4 %collective-permute-start.10 = (f32[288,512]{1,0:T(8,128)}, f32[288,512]{1,0:T(8,128)S(1)}, u32[]{:S(2)}, u32[]{:S(2)}) collective-permute-start(f32[288,512]{1,0:T(8,128)} %get-tuple-element.14), channel_id=1, source_target_pairs={{0,4},{1,5},{2,6},{3,7}} | collective-permute-start | bytes 1769480 | tf_op jit(solution)/shard_map/ppermute | solution.py:437
  5.9 1.8 %collective-permute-done.10.refs_1_ = f32[288,512]{1,0:T(8,128)S(1)} collective-permute-done((f32[288,512]{1,0:T(8,128)}, f32[288,512]{1,0:T(8,128)S(1)}, u32[]{:S(2)}, u32[]{:S(2)}) %collective-permute-start.10) | collective-permute-done | bytes 589856 | tf_op jit(solution)/shard_map/ppermute | solution.py:437
  7.7 0.0 copy-start.1
  7.7 1.1 %copy-done.1 = f32[288,512]{1,0:T(8,128)S(1)} copy-done((f32[288,512]{1,0:T(8,128)S(1)}, f32[288,512]{1,0:T(8,128)}, u32[]{:S(2)}) %copy-start.1) | copy-done | bytes 589848
  8.8 0.1 shard_map.45.refs_0_
  8.9 1.4 %collective-permute-start.11 = (f32[288,512]{1,0:T(8,128)S(1)}, f32[288,512]{1,0:T(8,128)S(1)}, u32[]{:S(2)}, u32[]{:S(2)}) collective-permute-start(f32[288,512]{1,0:T(8,128)S(1)} %shard_map.45.refs_0_), channel_id=1, source_target_pairs={{0,16},{1,17},{2,18},{3,19},{4,12},{5,13},{6,14},{7,15}} | collective-permute-start | bytes 1769480 | tf_op jit(solution)/shard_map/ppermute | solution.py:437
  10.3 4.2 %collective-permute-start = (f32[128,384]{1,0:T(8,128)}, f32[128,384]{1,0:T(8,128)S(1)}, u32[]{:S(2)}, u32[]{:S(2)}) collective-permute-start(f32[128,384]{1,0:T(8,128)} %get-tuple-element.11.refs_0_), channel_id=1, source_target_pairs={{0,1}} | collective-permute-start | bytes 589832 | tf_op jit(solution)/shard_map/ppermute | solution.py:437
  14.5 1.7 %collective-permute-start.1 = (f32[128,384]{1,0:T(8,128)}, f32[128,384]{1,0:T(8,128)S(1)}, u32[]{:S(2)}, u32[]{:S(2)}) collective-permute-start(f32[128,384]{1,0:T(8,128)} %get-tuple-element.11.refs_0_), channel_id=1, source_target_pairs={{0,2}} | collective-permute-start | bytes 589832 | tf_op jit(solution)/shard_map/ppermute | solution.py:437
  16.2 1.7 %collective-permute-start.2 = (f32[128,384]{1,0:T(8,128)}, f32[128,384]{1,0:T(8,128)S(1)}, u32[]{:S(2)}, u32[]{:S(2)}) collective-permute-start(f32[128,384]{1,0:T(8,128)} %get-tuple-element.11.refs_0_), channel_id=1, source_target_pairs={{0,3}} | collective-permute-start | bytes 589832 | tf_op jit(solution)/shard_map/ppermute | solution.py:437
  17.9 1.3 %collective-permute-start.12 = (f32[288,512]{1,0:T(8,128)S(1)}, f32[288,512]{1,0:T(8,128)S(1)}, u32[]{:S(2)}, u32[]{:S(2)}) collective-permute-start(f32[288,512]{1,0:T(8,128)S(1)} %shard_map.45.refs_0_), channel_id=1, source_target_pairs={{0,8},{1,9},{2,10},{3,11},{4,20},{5,21},{6,22},{7,23}} | collective-permute-start | bytes 1769480 | tf_op jit(solution)/shard_map/ppermute | solution.py:437
  19.3 1.8 %collective-permute-done.11.refs_1_ = f32[288,512]{1,0:T(8,128)S(1)} collective-permute-done((f32[288,512]{1,0:T(8,128)S(1)}, f32[288,512]{1,0:T(8,128)S(1)}, u32[]{:S(2)}, u32[]{:S(2)}) %collective-permute-start.11) | collective-permute-done | bytes 589856 | tf_op jit(solution)/shard_map/ppermute | solution.py:437
  21.0 0.7 %collective-permute-start.13 = (f32[288,512]{1,0:T(8,128)S(1)}, f32[288,512]{1,0:T(8,128)S(1)}, u32[]{:S(2)}, u32[]{:S(2)}) collective-permute-start(f32[288,512]{1,0:T(8,128)S(1)} %collective-permute-done.11.refs_1_), channel_id=1, source_target_pairs={{16,24},{17,25},{18,26},{19,27},{12,28},{13,29},{14,30},{15,31}} | collective-permute-start | bytes 1769480 | tf_op jit(solution)/shard_map/ppermute | solution.py:437
  21.7 0.0 collective-permute-done.refs_1_
  21.7 5.1 %collective-permute-start.7 = (f32[512,256]{1,0:T(8,128)}, f32[512,256]{1,0:T(8,128)S(1)}, u32[]{:S(2)}, u32[]{:S(2)}) collective-permute-start(f32[512,256]{1,0:T(8,128)} %get-tuple-element.12.refs_0_), channel_id=1, source_target_pairs={{0,2},{4,6},{8,10},{12,14},{16,17},{20,21},{24,25},{28,29}} | collective-permute-start | bytes 1572872 | tf_op jit(solution)/shard_map/ppermute | solution.py:437
  26.9 0.0 collective-permute-done.1.refs_2_
  26.9 0.0 collective-permute-done.2.refs_3_
  26.9 0.0 copy-start.4
  26.9 0.9 %copy-done.4 = f32[128,384]{1,0:T(8,128)S(1)} copy-done((f32[128,384]{1,0:T(8,128)S(1)}, f32[128,384]{1,0:T(8,128)}, u32[]{:S(2)}) %copy-start.4) | copy-done | bytes 196632
  27.8 6.8 %shard_map.42.refs_0_ = f32[128,384]{1,0:T(8,128)S(1)} custom-call(f32[128,384]{1,0:T(8,128)S(1)} %copy-done.4, f32[128,384]{1,0:T(8,128)S(1)} %collective-permute-done.refs_1_, f32[128,384]{1,0:T(8,128)S(1)} %collective-permute-done.1.refs_2_, f32[128,384]{1,0:T(8,128)S(1)} %collective-permute-done.2.refs_3_), custom_call_target="tpu_custom_call" | custom-call | flops 4294967296 | bytes 524288 | tf_op jit(solution)/shard_map/pallas_call | solution.py:137
  34.6 0.0 copy-start.2
  34.6 1.4 %collective-permute-start.3 = (f32[128,384]{1,0:T(8,128)S(1)}, f32[128,384]{1,0:T(8,128)S(1)}, u32[]{:S(2)}, u32[]{:S(2)}) collective-permute-start(f32[128,384]{1,0:T(8,128)S(1)} %shard_map.42.refs_0_), channel_id=1, source_target_pairs={{0,8},{1,9},{2,10},{3,11}} | collective-permute-start | bytes 589832 | tf_op jit(solution)/shard_map/ppermute | solution.py:437
  36.1 0.0 collective-permute-done.12.refs_2_
  36.1 0.0 collective-permute-done.13.refs_3_
  36.1 0.2 shard_map.46.refs_4_.refs_3_
  36.3 0.1 collective-permute-start.14
  36.3 0.0 copy-done.2
  36.4 1.3 %collective-permute-start.8 = (f32[512,256]{1,0:T(8,128)S(1)}, f32[512,256]{1,0:T(8,128)S(1)}, u32[]{:S(2)}, u32[]{:S(2)}) collective-permute-start(f32[512,256]{1,0:T(8,128)S(1)} %copy-done.2), channel_id=1, source_target_pairs={{0,1},{4,5},{8,11},{12,15},{16,19},{20,23},{24,26},{28,30}} | collective-permute-start | bytes 1572872 | tf_op jit(solution)/shard_map/ppermute | solution.py:437
  37.7 0.0 collective-permute-done.7.refs_1_
  37.7 0.7 %collective-permute-start.9 = (f32[512,256]{1,0:T(8,128)S(1)}, f32[512,256]{1,0:T(8,128)S(1)}, u32[]{:S(2)}, u32[]{:S(2)}) collective-permute-start(f32[512,256]{1,0:T(8,128)S(1)} %collective-permute-done.7.refs_1_), channel_id=1, source_target_pairs={{2,3},{6,7}} | collective-permute-start | bytes 1572872 | tf_op jit(solution)/shard_map/ppermute | solution.py:437
  38.4 4.8 %collective-permute-start.4 = (f32[128,384]{1,0:T(8,128)S(1)}, f32[128,384]{1,0:T(8,128)S(1)}, u32[]{:S(2)}, u32[]{:S(2)}) collective-permute-start(f32[128,384]{1,0:T(8,128)S(1)} %shard_map.42.refs_0_), channel_id=1, source_target_pairs={{0,16},{1,17},{2,18},{3,19}} | collective-permute-start | bytes 589832 | tf_op jit(solution)/shard_map/ppermute | solution.py:437
  43.2 0.0 collective-permute-done.3.refs_1_
  43.2 1.3 %collective-permute-start.5 = (f32[128,384]{1,0:T(8,128)S(1)}, f32[128,384]{1,0:T(8,128)S(1)}, u32[]{:S(2)}, u32[]{:S(2)}) collective-permute-start(f32[128,384]{1,0:T(8,128)S(1)} %shard_map.42.refs_0_), channel_id=1, source_target_pairs={{0,24},{1,25},{2,26},{3,27}} | collective-permute-start | bytes 589832 | tf_op jit(solution)/shard_map/ppermute | solution.py:437
  44.5 1.8 %collective-permute-done.4.refs_2_ = f32[128,384]{1,0:T(8,128)S(1)} collective-permute-done((f32[128,384]{1,0:T(8,128)S(1)}, f32[128,384]{1,0:T(8,128)S(1)}, u32[]{:S(2)}, u32[]{:S(2)}) %collective-permute-start.4) | collective-permute-done | bytes 196640 | tf_op jit(solution)/shard_map/ppermute | solution.py:437
  46.3 1.3 %collective-permute-done.5.refs_3_ = f32[128,384]{1,0:T(8,128)S(1)} collective-permute-done((f32[128,384]{1,0:T(8,128)S(1)}, f32[128,384]{1,0:T(8,128)S(1)}, u32[]{:S(2)}, u32[]{:S(2)}) %collective-permute-start.5) | collective-permute-done | bytes 196640 | tf_op jit(solution)/shard_map/ppermute | solution.py:437
  47.7 0.0 copy-start.3
  47.7 1.4 %collective-permute-start.6 = (f32[128,384]{1,0:T(8,128)S(1)}, f32[128,384]{1,0:T(8,128)S(1)}, u32[]{:S(2)}, u32[]{:S(2)}) collective-permute-start(f32[128,384]{1,0:T(8,128)S(1)} %shard_map.43.refs_0_), channel_id=1, source_target_pairs={{0,4},{1,5},{2,6},{3,7},{8,12},{9,13},{10,14},{11,15},{16,20},{17,... | collective-permute-start | bytes 589832 | tf_op jit(solution)/shard_map/ppermute | solution.py:437
  49.2 1.0 %collective-permute-done.6.refs_1_ = f32[128,384]{1,0:T(8,128)S(1)} collective-permute-done((f32[128,384]{1,0:T(8,128)S(1)}, f32[128,384]{1,0:T(8,128)S(1)}, u32[]{:S(2)}, u32[]{:S(2)}) %collective-permute-start.6) | collective-permute-done | bytes 196640 | tf_op jit(solution)/shard_map/ppermute | solution.py:437
  50.2 0.0 collective-permute-done.8.refs_2_
  50.2 0.0 collective-permute-done.9.refs_3_
  50.2 0.1 shard_map.47.refs_1_
  50.3 0.0 copy-start
  50.3 0.0 collective-permute-done.14.refs_4_
  50.3 0.0 copy-done.3
  50.3 2.4 %shard_map.48 = (f32[512,256]{1,0:T(8,128)S(1)}, f32[128,128]{1,0:T(8,128)S(1)}, f32[128,128]{1,0:T(8,128)S(1)}, f32[128,128]{1,0:T(8,128)S(1)}, f32[128,128]{1,0:T(8,128)S(1)}) custom-call(f32[128,384]{1,0:T(8,128)S(1)} %shard_map.44.refs_0_, f32[512,256]{1,0:T(8,128)S(1)} %shard_map.47.refs_1_, f32[512,128]{1,0:T(8,128)S(1)} %copy-done.3, ...), custom_call_target="tpu_custom_call" | custom-call | flops 1073741824 | bytes 2097152 | tf_op jit(solution)/shard_map/pallas_call | solution.py:322
  52.7 2.8 %collective-permute-start.15 = (f32[128,128]{1,0:T(8,128)S(1)}, f32[128,128]{1,0:T(8,128)S(1)}, u32[]{:S(2)}, u32[]{:S(2)}) collective-permute-start(f32[128,128]{1,0:T(8,128)S(1)} %get-tuple-element.16), channel_id=1, source_target_pairs={{0,3},{1,2},{2,1},{3,0},{4,7},{5,6},{6,5},{7,4},{8,11},{9,10},{10,... | collective-permute-start | bytes 196616 | tf_op jit(solution)/shard_map/ppermute | solution.py:437
  55.6 0.7 %collective-permute-start.16 = (f32[128,128]{1,0:T(8,128)S(1)}, f32[128,128]{1,0:T(8,128)S(1)}, u32[]{:S(2)}, u32[]{:S(2)}) collective-permute-start(f32[128,128]{1,0:T(8,128)S(1)} %get-tuple-element.17), channel_id=1, source_target_pairs={{0,2},{1,3},{2,0},{3,1},{4,6},{5,7},{6,4},{7,5},{8,10},{9,11},{10,... | collective-permute-start | bytes 196616 | tf_op jit(solution)/shard_map/ppermute | solution.py:437
  56.2 1.0 %collective-permute-start.17 = (f32[128,128]{1,0:T(8,128)S(1)}, f32[128,128]{1,0:T(8,128)S(1)}, u32[]{:S(2)}, u32[]{:S(2)}) collective-permute-start(f32[128,128]{1,0:T(8,128)S(1)} %get-tuple-element.18), channel_id=1, source_target_pairs={{0,1},{1,0},{2,3},{3,2},{4,5},{5,4},{6,7},{7,6},{8,9},{9,8},{10,11... | collective-permute-start | bytes 196616 | tf_op jit(solution)/shard_map/ppermute | solution.py:437
  57.2 0.0 copy-done
  57.2 4.3 %shard_map.49 = f32[512,1024]{1,0:T(8,128)} custom-call(f32[128,384]{1,0:T(8,128)S(1)} %shard_map.44.refs_0_, f32[512,256]{1,0:T(8,128)S(1)} %get-tuple-element.15.refs_1_, f32[512,1024]{1,0:T(8,128)S(1)} %copy-done, f32[288,512]{1,0:T(8,128)S(1)} %shard_map.46.refs_4_.refs_3_, f32[288,512]{1,0:T(8,128)} %collective-permute-done.14.refs_4_), custom_call_target="tpu_custom_call" | custom-call | flops 2147483648 | bytes 6291456 | tf_op jit(solution)/shard_map/pallas_call | solution.py:374
  61.5 0.0 collective-permute-done.15
  61.5 0.9 %collective-permute-done.16 = f32[128,128]{1,0:T(8,128)S(1)} collective-permute-done((f32[128,128]{1,0:T(8,128)S(1)}, f32[128,128]{1,0:T(8,128)S(1)}, u32[]{:S(2)}, u32[]{:S(2)}) %collective-permute-start.16) | collective-permute-done | bytes 65568 | tf_op jit(solution)/shard_map/ppermute | solution.py:437
  62.3 0.0 collective-permute-done.17
  62.4 0.7 %pad_maximum_fusion = f32[128,512]{1,0:T(8,128)} fusion(f32[128,128]{1,0:T(8,128)S(1)} %get-tuple-element.21, f32[128,128]{1,0:T(8,128)S(1)} %get-tuple-element.22, f32[128,128]{1,0:T(8,128)S(1)} %get-tuple-element.23, f32[128,128]{1,0:T(8,128)S(1)} %get-tuple-element.20), kind=kLoop, calls=%fused_computation | loop fusion | flops 196608 | bytes 524288 | tf_op jit(solution)/shard_map/concatenate | solution.py:526
  (3 shorter events, 0.1 us)
Async XLA Ops:
  3.5 4.2 %collective-permute-start.10 = (f32[288,512]{1,0:T(8,128)}, f32[288,512]{1,0:T(8,128)S(1)}, u32[]{:S(2)}, u32[]{:S(2)}) collective-permute-start(f32[288,512]{1,0:T(8,128)} %get-tuple-element.14), channel_id=1, source_target_pairs={{0,4},{1,5},{2,6},{3,7}} | collective-permute-start | bytes 1769480 | tf_op jit(solution)/shard_map/ppermute | solution.py:437
  7.7 1.1 %copy-start.1 = (f32[288,512]{1,0:T(8,128)S(1)}, f32[288,512]{1,0:T(8,128)}, u32[]{:S(2)}) copy-start(f32[288,512]{1,0:T(8,128)} %get-tuple-element.13.refs_0_) | copy-start | bytes 1769476
  8.9 12.1 %collective-permute-start.11 = (f32[288,512]{1,0:T(8,128)S(1)}, f32[288,512]{1,0:T(8,128)S(1)}, u32[]{:S(2)}, u32[]{:S(2)}) collective-permute-start(f32[288,512]{1,0:T(8,128)S(1)} %shard_map.45.refs_0_), channel_id=1, source_target_pairs={{0,16},{1,17},{2,18},{3,19},{4,12},{5,13},{6,14},{7,15}} | collective-permute-start | bytes 1769480 | tf_op jit(solution)/shard_map/ppermute | solution.py:437
  10.3 11.4 %collective-permute-start = (f32[128,384]{1,0:T(8,128)}, f32[128,384]{1,0:T(8,128)S(1)}, u32[]{:S(2)}, u32[]{:S(2)}) collective-permute-start(f32[128,384]{1,0:T(8,128)} %get-tuple-element.11.refs_0_), channel_id=1, source_target_pairs={{0,1}} | collective-permute-start | bytes 589832 | tf_op jit(solution)/shard_map/ppermute | solution.py:437
  14.5 12.3 %collective-permute-start.1 = (f32[128,384]{1,0:T(8,128)}, f32[128,384]{1,0:T(8,128)S(1)}, u32[]{:S(2)}, u32[]{:S(2)}) collective-permute-start(f32[128,384]{1,0:T(8,128)} %get-tuple-element.11.refs_0_), channel_id=1, source_target_pairs={{0,2}} | collective-permute-start | bytes 589832 | tf_op jit(solution)/shard_map/ppermute | solution.py:437
  16.2 10.7 %collective-permute-start.2 = (f32[128,384]{1,0:T(8,128)}, f32[128,384]{1,0:T(8,128)S(1)}, u32[]{:S(2)}, u32[]{:S(2)}) collective-permute-start(f32[128,384]{1,0:T(8,128)} %get-tuple-element.11.refs_0_), channel_id=1, source_target_pairs={{0,3}} | collective-permute-start | bytes 589832 | tf_op jit(solution)/shard_map/ppermute | solution.py:437
  17.9 18.1 %collective-permute-start.12 = (f32[288,512]{1,0:T(8,128)S(1)}, f32[288,512]{1,0:T(8,128)S(1)}, u32[]{:S(2)}, u32[]{:S(2)}) collective-permute-start(f32[288,512]{1,0:T(8,128)S(1)} %shard_map.45.refs_0_), channel_id=1, source_target_pairs={{0,8},{1,9},{2,10},{3,11},{4,20},{5,21},{6,22},{7,23}} | collective-permute-start | bytes 1769480 | tf_op jit(solution)/shard_map/ppermute | solution.py:437
  21.0 15.0 %collective-permute-start.13 = (f32[288,512]{1,0:T(8,128)S(1)}, f32[288,512]{1,0:T(8,128)S(1)}, u32[]{:S(2)}, u32[]{:S(2)}) collective-permute-start(f32[288,512]{1,0:T(8,128)S(1)} %collective-permute-done.11.refs_1_), channel_id=1, source_target_pairs={{16,24},{17,25},{18,26},{19,27},{12,28},{13,29},{14,30},{15,31}} | collective-permute-start | bytes 1769480 | tf_op jit(solution)/shard_map/ppermute | solution.py:437
  21.7 15.9 %collective-permute-start.7 = (f32[512,256]{1,0:T(8,128)}, f32[512,256]{1,0:T(8,128)S(1)}, u32[]{:S(2)}, u32[]{:S(2)}) collective-permute-start(f32[512,256]{1,0:T(8,128)} %get-tuple-element.12.refs_0_), channel_id=1, source_target_pairs={{0,2},{4,6},{8,10},{12,14},{16,17},{20,21},{24,25},{28,29}} | collective-permute-start | bytes 1572872 | tf_op jit(solution)/shard_map/ppermute | solution.py:437
  26.9 0.9 %copy-start.4 = (f32[128,384]{1,0:T(8,128)S(1)}, f32[128,384]{1,0:T(8,128)}, u32[]{:S(2)}) copy-start(f32[128,384]{1,0:T(8,128)} %get-tuple-element.11.refs_0_) | copy-start | bytes 589828
  34.6 1.7 %copy-start.2 = (f32[512,256]{1,0:T(8,128)S(1)}, f32[512,256]{1,0:T(8,128)}, u32[]{:S(2)}) copy-start(f32[512,256]{1,0:T(8,128)} %get-tuple-element.12.refs_0_) | copy-start | bytes 1572868
  34.6 8.5 %collective-permute-start.3 = (f32[128,384]{1,0:T(8,128)S(1)}, f32[128,384]{1,0:T(8,128)S(1)}, u32[]{:S(2)}, u32[]{:S(2)}) collective-permute-start(f32[128,384]{1,0:T(8,128)S(1)} %shard_map.42.refs_0_), channel_id=1, source_target_pairs={{0,8},{1,9},{2,10},{3,11}} | collective-permute-start | bytes 589832 | tf_op jit(solution)/shard_map/ppermute | solution.py:437
  36.3 14.1 %collective-permute-start.14 = (f32[288,512]{1,0:T(8,128)S(1)}, f32[288,512]{1,0:T(8,128)}, u32[]{:S(2)}, u32[]{:S(2)}) collective-permute-start(f32[288,512]{1,0:T(8,128)S(1)} %shard_map.46.refs_4_.refs_3_), channel_id=1, source_target_pairs={{0,4},{4,0},{1,5},{5,1},{2,6},{6,2},{3,7},{7,3},{8,12},{12,8},{9,1... | collective-permute-start | bytes 1769480 | tf_op jit(solution)/shard_map/ppermute | solution.py:437
  36.4 13.8 %collective-permute-start.8 = (f32[512,256]{1,0:T(8,128)S(1)}, f32[512,256]{1,0:T(8,128)S(1)}, u32[]{:S(2)}, u32[]{:S(2)}) collective-permute-start(f32[512,256]{1,0:T(8,128)S(1)} %copy-done.2), channel_id=1, source_target_pairs={{0,1},{4,5},{8,11},{12,15},{16,19},{20,23},{24,26},{28,30}} | collective-permute-start | bytes 1572872 | tf_op jit(solution)/shard_map/ppermute | solution.py:437
  37.7 12.5 %collective-permute-start.9 = (f32[512,256]{1,0:T(8,128)S(1)}, f32[512,256]{1,0:T(8,128)S(1)}, u32[]{:S(2)}, u32[]{:S(2)}) collective-permute-start(f32[512,256]{1,0:T(8,128)S(1)} %collective-permute-done.7.refs_1_), channel_id=1, source_target_pairs={{2,3},{6,7}} | collective-permute-start | bytes 1572872 | tf_op jit(solution)/shard_map/ppermute | solution.py:437
  38.4 7.9 %collective-permute-start.4 = (f32[128,384]{1,0:T(8,128)S(1)}, f32[128,384]{1,0:T(8,128)S(1)}, u32[]{:S(2)}, u32[]{:S(2)}) collective-permute-start(f32[128,384]{1,0:T(8,128)S(1)} %shard_map.42.refs_0_), channel_id=1, source_target_pairs={{0,16},{1,17},{2,18},{3,19}} | collective-permute-start | bytes 589832 | tf_op jit(solution)/shard_map/ppermute | solution.py:437
  43.2 4.5 %collective-permute-start.5 = (f32[128,384]{1,0:T(8,128)S(1)}, f32[128,384]{1,0:T(8,128)S(1)}, u32[]{:S(2)}, u32[]{:S(2)}) collective-permute-start(f32[128,384]{1,0:T(8,128)S(1)} %shard_map.42.refs_0_), channel_id=1, source_target_pairs={{0,24},{1,25},{2,26},{3,27}} | collective-permute-start | bytes 589832 | tf_op jit(solution)/shard_map/ppermute | solution.py:437
  47.7 2.7 %copy-start.3 = (f32[512,128]{1,0:T(8,128)S(1)}, f32[512,128]{1,0:T(8,128)}, u32[]{:S(2)}) copy-start(f32[512,128]{1,0:T(8,128)} %refs_2_.2) | copy-start | bytes 786436
  47.7 2.5 %collective-permute-start.6 = (f32[128,384]{1,0:T(8,128)S(1)}, f32[128,384]{1,0:T(8,128)S(1)}, u32[]{:S(2)}, u32[]{:S(2)}) collective-permute-start(f32[128,384]{1,0:T(8,128)S(1)} %shard_map.43.refs_0_), channel_id=1, source_target_pairs={{0,4},{1,5},{2,6},{3,7},{8,12},{9,13},{10,14},{11,15},{16,20},{17,... | collective-permute-start | bytes 589832 | tf_op jit(solution)/shard_map/ppermute | solution.py:437
  50.3 6.9 %copy-start = (f32[512,1024]{1,0:T(8,128)S(1)}, f32[512,1024]{1,0:T(8,128)}, u32[]{:S(2)}) copy-start(f32[512,1024]{1,0:T(8,128)} %refs_2_.3) | copy-start | bytes 6291460
  52.7 8.7 %collective-permute-start.15 = (f32[128,128]{1,0:T(8,128)S(1)}, f32[128,128]{1,0:T(8,128)S(1)}, u32[]{:S(2)}, u32[]{:S(2)}) collective-permute-start(f32[128,128]{1,0:T(8,128)S(1)} %get-tuple-element.16), channel_id=1, source_target_pairs={{0,3},{1,2},{2,1},{3,0},{4,7},{5,6},{6,5},{7,4},{8,11},{9,10},{10,... | collective-permute-start | bytes 196616 | tf_op jit(solution)/shard_map/ppermute | solution.py:437
  55.6 6.8 %collective-permute-start.16 = (f32[128,128]{1,0:T(8,128)S(1)}, f32[128,128]{1,0:T(8,128)S(1)}, u32[]{:S(2)}, u32[]{:S(2)}) collective-permute-start(f32[128,128]{1,0:T(8,128)S(1)} %get-tuple-element.17), channel_id=1, source_target_pairs={{0,2},{1,3},{2,0},{3,1},{4,6},{5,7},{6,4},{7,5},{8,10},{9,11},{10,... | collective-permute-start | bytes 196616 | tf_op jit(solution)/shard_map/ppermute | solution.py:437
  56.2 6.1 %collective-permute-start.17 = (f32[128,128]{1,0:T(8,128)S(1)}, f32[128,128]{1,0:T(8,128)S(1)}, u32[]{:S(2)}, u32[]{:S(2)}) collective-permute-start(f32[128,128]{1,0:T(8,128)S(1)} %get-tuple-element.18), channel_id=1, source_target_pairs={{0,1},{1,0},{2,3},{3,2},{4,5},{5,4},{6,7},{7,6},{8,9},{9,8},{10,11... | collective-permute-start | bytes 196616 | tf_op jit(solution)/shard_map/ppermute | solution.py:437
